TPU v7x, 256 devices: a whole 4x4x8 slice. The times are simulated.
256 devices in a mesh: dp: 16 (over x, z_hi, core), ctx: 16 (over z_lo, y).
Axes of the slice: x: 4, y: 4, z: 8 (z_hi: 2, z_lo: 4; z = z_hi * 4 + z_lo), core: 2. Of those that a mesh axis runs over, the one named last changes fastest.
Arguments:
- tokens: bfloat16 [16, 4096, 2560], P('dp', 'ctx'), may hold values from -6 to 6
- w_x: bfloat16 [2560, 2560], P(None, 'dp'), may hold values from -0.125 to 0.125
- w_bc: bfloat16 [2560, 256], replicated, may hold values from -0.009765625 to 0.009765625
- w_dt: bfloat16 [2560, 40], replicated, may hold values from -0.125 to 0.125
- dt_bias: float32 [40], replicated, may hold values from -1 to 1
- decay_rate: float32 [40], replicated, may hold values from 0.00012207031 to 0.08
- skip_gain: float32 [40], replicated, may hold values from 0.5 to 1.5
- grad_y: bfloat16 [16, 4096, 2560], P('dp', 'ctx'), may hold values from -6 to 6
Outputs:
- head_out: bfloat16 [16, 4096, 2560], P('dp', 'ctx')
- d_tokens: bfloat16 [16, 4096, 2560], P('dp', 'ctx')
All inputs are finite; a program needn't handle non-finite values.
Results may differ from a plain program's by a relative error of at most 0.017.
Values may be sent and summed in bfloat16 or wider, within the bound.
A program may use at most 128 MiB of HBM per device.

v0:
```python
import jax
import jax.numpy as jnp
from jax import lax
from jax.sharding import PartitionSpec as P

Q = 256


HIGHEST_PRECISION = lax.Precision.HIGHEST


def prefix(value, axis, combine, identity, reverse):
    peers, mine = (lax.axis_size(axis), lax.axis_index(axis))
    everything = jax.tree.map(
        lambda part, kind: lax.all_gather(part.astype(kind), axis),
        value,
        (jnp.bfloat16, jnp.bfloat16),
    )
    start = jax.tree.map(
        lambda part, zero: jnp.broadcast_to(jnp.asarray(zero, part.dtype), part.shape),
        value,
        identity,
    )

    def lap(k, before):
        at = peers - 1 - k if reverse else k
        reached = at > mine if reverse else at < mine
        new = combine(
            before, jax.tree.map(lambda part, own: part[at].astype(own.dtype), everything, value)
        )
        return jax.tree.map(lambda a, b: jnp.where(reached, a, b), new, before)

    return lax.fori_loop(0, peers, lap, start)


def group_rates(raw_block, rate_vec, bias_vec):
    step_size = jax.nn.softplus(raw_block + bias_vec[None, :])
    running = jnp.cumsum(-rate_vec[None, :] * step_size, axis=0)
    return (step_size, running)


def group_forward(entering, pieces, rate_vec, bias_vec, skip_vec):
    x_block, raw_block, b_block, c_block = pieces
    step_size, running = group_rates(raw_block, rate_vec, bias_vec)
    length = x_block.shape[0]
    scores = jnp.dot(
        c_block.astype(jnp.bfloat16),
        b_block.astype(jnp.bfloat16).T,
        preferred_element_type=jnp.float32,
    )
    causal = jnp.arange(length)[:, None] >= jnp.arange(length)[None, :]
    by_head = running.T
    spread = by_head[:, :, None] - by_head[:, None, :]
    decays = jnp.exp(jnp.where(causal[None, :, :], spread, -1e30))
    mixing = scores[None, :, :] * decays * step_size.T[:, None, :]
    within = jnp.einsum("hij,jhp->ihp", mixing, x_block, precision=HIGHEST_PRECISION)
    carried = (
        jnp.einsum("in,hpn->ihp", c_block, entering, precision=HIGHEST_PRECISION)
        * jnp.exp(running)[:, :, None]
    )
    outputs = within + carried + skip_vec[None, :, None] * x_block
    weights_tail = jnp.exp(running[-1][None, :] - running) * step_size
    updated = jnp.exp(running[-1])[:, None, None] * entering + jnp.einsum(
        "jh,jhp,jn->hpn", weights_tail, x_block, b_block, precision=HIGHEST_PRECISION
    )
    return (updated, outputs)


def split_blocks(array, count):
    return array.reshape((count, array.shape[0] // count) + array.shape[1:])


def run_block(values, entering, rate_vec, bias_vec, skip_vec):
    x_all = values[0]
    count = x_all.shape[0] // Q

    def run_advance(carried_in, pieces):
        return group_forward(carried_in, pieces, rate_vec, bias_vec, skip_vec)

    final_state, outputs = lax.scan(
        run_advance, entering, tuple((split_blocks(member, count) for member in values))
    )
    return (outputs.reshape(x_all.shape), final_state)


def block_state(x_all, raw_all, b_all, rate_vec, bias_vec):
    count = x_all.shape[0] // Q

    def block_advance(entering, pieces):
        x_block, raw_block, b_block = pieces
        step_size, running = group_rates(raw_block, rate_vec, bias_vec)
        weights_tail = jnp.exp(running[-1][None, :] - running) * step_size
        updated = jnp.exp(running[-1])[:, None, None] * entering + jnp.einsum(
            "jh,jhp,jn->hpn", weights_tail, x_block, b_block, precision=HIGHEST_PRECISION
        )
        return (updated, running[-1])

    zero_state = jnp.zeros((x_all.shape[1], x_all.shape[2], b_all.shape[1]), jnp.float32)
    final_state, totals = lax.scan(
        block_advance,
        zero_state,
        (split_blocks(x_all, count), split_blocks(raw_all, count), split_blocks(b_all, count)),
    )
    return (jnp.exp(jnp.sum(totals, axis=0)), final_state)


def combine_states(earlier, later):
    return (earlier[0] * later[0], later[0][:, None, None] * earlier[1] + later[1])


def combine_grads(earlier, later):
    return (earlier[0] * later[0], later[1] + later[0][:, None, None] * earlier[1])


def local(tokens, w_x, w_bc, w_dt, dt_bias, decay_rate, skip_gain, grad_y):
    tok_rows = tokens[0]
    steps_here = tok_rows.shape[0]
    head_count = dt_bias.shape[0]
    width_hp = grad_y.shape[2]
    head_size = width_hp // head_count
    state_size = w_bc.shape[1] // 2
    contract = (((1,), (1,)), ((), ()))
    full_panel = lax.all_gather(w_x, "dp", axis=1, tiled=True)
    x_round = jnp.dot(tok_rows, full_panel, preferred_element_type=jnp.float32).astype(jnp.bfloat16)
    bc_round = jnp.dot(tok_rows, w_bc, preferred_element_type=jnp.float32).astype(jnp.bfloat16)
    raw_dt = jnp.dot(tok_rows, w_dt, preferred_element_type=jnp.float32)
    x_float = (
        lax.optimization_barrier(x_round)
        .astype(jnp.float32)
        .reshape(steps_here, head_count, head_size)
    )
    bc_float = lax.optimization_barrier(bc_round).astype(jnp.float32)
    b_float = bc_float[:, :state_size]
    c_float = bc_float[:, state_size:]
    grad_float = grad_y[0].astype(jnp.float32).reshape(steps_here, head_count, head_size)
    decay_total, local_state = block_state(x_float, raw_dt, b_float, decay_rate, dt_bias)
    step_size = jax.nn.softplus(raw_dt + dt_bias[None, :])
    running = jnp.cumsum(-decay_rate[None, :] * step_size, axis=0)
    direct_grad = jnp.einsum(
        "th,thp,tn->hpn", jnp.exp(running), grad_float, c_float, precision=HIGHEST_PRECISION
    )
    unit_decay = jnp.ones_like(decay_total)
    zero_state = jnp.zeros_like(local_state)
    entering = prefix(
        (decay_total, local_state), "ctx", combine_states, (unit_decay, zero_state), False
    )[1]
    later_grad = prefix(
        (decay_total, direct_grad), "ctx", combine_grads, (unit_decay, zero_state), True
    )[1]

    def forward(x_arg, raw_arg, b_arg, c_arg):
        return run_block((x_arg, raw_arg, b_arg, c_arg), entering, decay_rate, dt_bias, skip_gain)

    (head_float, final_state), backward = jax.vjp(forward, x_float, raw_dt, b_float, c_float)
    grad_x, grad_raw, grad_b, grad_c = backward((grad_float, later_grad))
    grad_x_round = grad_x.reshape(steps_here, width_hp).astype(jnp.bfloat16)
    grad_bc_round = jnp.concatenate([grad_b, grad_c], axis=1).astype(jnp.bfloat16)
    grad_raw_round = grad_raw.astype(jnp.bfloat16)
    total = lax.dot_general(grad_x_round, full_panel, contract, preferred_element_type=jnp.float32)
    total = total + lax.dot_general(
        grad_bc_round, w_bc, contract, preferred_element_type=jnp.float32
    )
    total = total + lax.dot_general(
        grad_raw_round, w_dt, contract, preferred_element_type=jnp.float32
    )
    head_out = head_float.reshape(steps_here, width_hp).astype(jnp.bfloat16)
    return (head_out[None], total.astype(jnp.bfloat16)[None])


def solution(mesh):
    placed = (P("dp", "ctx", None), P(None, "dp"), P(), P(), P(), P(), P(), P("dp", "ctx", None))
    return jax.shard_map(
        local,
        mesh=mesh,
        in_specs=placed,
        out_specs=(P("dp", "ctx", None), P("dp", "ctx", None)),
        check_vma=False,
    )
```

profile of v0, /device:TPU:2, one launch (start us, length us, event | category | flops | bytes accessed | tf_op | source)
XLA Modules:
  0.0 483.0 jit_solution(281639778616257343)
XLA Ops:
  7.2 0.8 neg.45
  8.0 0.5 copy-done
  8.5 1.4 fusion.61
  10.0 0.6 reduce-window.30
  10.9 1.8 fusion.51
  12.7 1.6 copy.35
  14.4 2.3 fusion.42
  16.7 0.7 all-gather.7.cloned.1.call-update
  17.7 43.8 %all-gather.2 = bf16[16,1,40]{2,1,0:T(2,128)(2,1)S(1)} all-gather(bf16[1,1,40]{2,1,0:T(2,128)(2,1)S(1)} %bitcast.230), channel_id=1, replica_groups=mesh['dp'=16,'ctx'=16] {'ctx'}, dimensions={0}, use_global_device_ids=true | all-gather | bytes 1360 | tf_op jit(solution)/shard_map/all_gather | solution.py:15
  61.7 81.7 %all-gather.11.cloned.1.call-done = bf16[640,64,128]{2,1,0:T(8,128)(2,1)} async-done(((bf16[40,64,128]{2,1,0:T(8,128)(2,1)}), bf16[640,64,128]{2,1,0:T(8,128)(2,1)}) %all-gather.11.cloned.1.call-update) | async-done | bytes 10485776 | tf_op jit(solution)/shard_map/all_gather | solution.py:15
  143.4 23.7 %while.23 = (s32[]{:T(128)}, f32[40,64,128]{2,1,0:T(8,128)S(1)}, s32[]{:T(128)}, bf16[16,40,64,128]{3,2,1,0:T(8,128)(2,1)}, bf16[16,40]{1,0:T(8,128)(2,1)S(1)}, ...) while((s32[]{:T(128)}, f32[40,64,128]{2,1,0:T(8,128)S(1)}, s32[]{:T(128)}, ...), condition=%wide.region_5.6_spmd.clone, body=%wide.region_4.5_spmd.clone.sunk | while | flops 1638448 | bytes 3277367 | solution.py:33
  143.4 1.4 fusion.134
  144.9 1.4 fusion.134
  146.4 1.4 fusion.134
  147.8 1.4 fusion.134
  149.3 1.4 fusion.134
  150.8 1.4 fusion.134
  152.2 1.4 fusion.134
  153.7 1.5 fusion.134
  155.2 1.5 fusion.134
  156.8 1.5 fusion.134
  158.4 1.4 fusion.134
  159.9 1.4 fusion.134
  161.3 1.4 fusion.134
  162.8 1.4 fusion.134
  164.3 1.4 fusion.134
  165.7 1.4 fusion.134
  167.2 119.7 %all-gather.7.cloned.1.call-done = bf16[2560,2560]{0,1:T(8,128)(2,1)} async-done(((bf16[2560,160]{0,1:T(8,128)(2,1)}), bf16[2560,2560]{0,1:T(8,128)(2,1)}) %all-gather.7.cloned.1.call-update) | async-done | bytes 13107216 | tf_op jit(solution)/shard_map/all_gather | solution.py:123
  286.9 9.4 %convolution_convert_fusion = bf16[256,2560]{1,0:T(8,128)(2,1)} fusion(bf16[2560,2560]{0,1:T(8,128)(2,1)} %all-gather.7.cloned.1.call-done, bf16[1,256,2560]{2,1,0:T(8,128)(2,1)S(1)} %copy-done), kind=kOutput, calls=%fused_computation.39 | convolution fusion | flops 3356098560 | bytes 15728640 | tf_op jit(solution)/shard_map/dot_general | solution.py:124
  296.3 2.4 copy.34
  298.7 4.1 fusion.30
  303.0 2.3 fusion.41
  305.3 3.0 bitcast_multiply_fusion.2
  308.7 9.3 %fusion.10 = (f32[40,256]{1,0:T(8,128)}, f32[40,256]{1,0:T(8,128)}, f32[40,256]{1,0:T(8,128)}, bf16[256,256]{1,0:T(8,128)(2,1)S(1)}) fusion(f32[40,256]{1,0:T(8,128)S(1)} %get-tuple-element.612, f32[40,256]{1,0:T(8,128)S(1)} %get-tuple-element.610, f32[256,256]{1,0:T(8,128)S(1)} %fusion.76, pred[256,256]{1,0:T(8,128)(4,1)S(1)} %iota_compare_fusion, ...), kind=kOutput, calls=%fused_computation.17 | convolution fusion | flops 369526784 | bytes 3284992 | tf_op jit(solution)/shard_map/transpose(jvp())/while/body/eval_jaxpr/hij,jhp->ihp/dot_general | solution.py:56
  318.5 2.5 fusion.58
  321.1 7.3 %fusion.34 = bf16[256,40,64]{0,2,1:T(8,128)(2,1)S(1)} fusion(bf16[256,40,64]{0,2,1:T(8,128)(2,1)S(1)} %bitcast.214, f32[256,40,64]{0,2,1:T(8,128)S(1)} %copy-done.9, bf16[40,64,256]{2,1,0:T(8,128)(2,1)S(1)} %bitcast.215, f32[40,256]{1,0:T(8,128)S(1)} %copy-done.17, f32[40,256]{1,0:T(8,128)S(1)} %copy-done.15, f32[256,256]{1,0:T(8,128)S(1)} %fusion.76, ...), kind=kOutput, calls=%fused_computation.49 | convolution fusion | flops 2027683840 | bytes 7004320 | tf_op jit(solution)/shard_map/transpose(jvp())/while/body/eval_jaxpr/hij,jhp->ihp/dot_general | solution.py:56
  328.5 5.2 %fusion.111 = f32[256,2560]{1,0:T(8,128)} fusion(bf16[256,2560]{0,1:T(8,128)(2,1)S(1)} %bitcast.223, bf16[2560,2560]{0,1:T(8,128)(2,1)S(1)} %bitcast.211), kind=kOutput, calls=%fused_computation.148 | convolution fusion | flops 3355443200 | bytes 17039360 | tf_op jit(solution)/shard_map/dot_general | solution.py:159
  333.7 91.2 %all-gather.9.cloned.1.call-done = bf16[640,64,128]{2,1,0:T(8,128)(2,1)} async-done(((bf16[40,64,128]{2,1,0:T(8,128)(2,1)}), bf16[640,64,128]{2,1,0:T(8,128)(2,1)}) %all-gather.9.cloned.1.call-update) | async-done | bytes 10485776 | tf_op jit(solution)/shard_map/all_gather | solution.py:15
  424.9 23.3 %while.22 = (s32[]{:T(128)}, f32[40,64,128]{2,1,0:T(8,128)S(1)}, s32[]{:T(128)}, bf16[16,40]{1,0:T(8,128)(2,1)S(1)}, bf16[16,40,64,128]{3,2,1,0:T(8,128)(2,1)}, /*index=5*/s32[]{:T(128)}, s32[]{:T(128)}) while((s32[]{:T(128)}, f32[40,64,128]{2,1,0:T(8,128)S(1)}, s32[]{:T(128)}, bf16[16,40]{1,0:T(8,128)(2,1)S(1)}, ...), condition=%wide.region_3.4_spmd.clone, body=%wide.region_2.3_spmd.clone.sunk | while | flops 1638444 | bytes 3277305 | solution.py:33
  424.9 1.4 fusion.133
  426.3 1.4 fusion.133
  427.8 1.4 fusion.133
  429.3 1.4 fusion.133
  430.7 1.4 fusion.133
  432.2 1.4 fusion.133
  433.6 1.4 fusion.133
  435.1 1.4 fusion.133
  436.5 1.4 fusion.133
  438.0 1.4 fusion.133
  439.5 1.4 fusion.133
  440.9 1.4 fusion.133
  442.4 1.4 fusion.133
  443.8 1.4 fusion.133
  445.3 1.4 fusion.133
  446.8 1.4 fusion.133
  448.2 1.8 multiply_reduce_fusion.1
  450.0 2.8 fusion.35
  452.9 0.9 copy_bitcast_fusion.1
  453.8 2.5 reduce-window.32
  456.5 10.9 %fusion.29 = bf16[256,40,64]{0,2,1:T(8,128)(2,1)} fusion(bf16[256,40,64]{0,2,1:T(8,128)(2,1)} %bitcast.219, f32[256,40,64]{0,2,1:T(8,128)} %get-tuple-element.617, f32[40,256]{1,0:T(8,128)} %copy-done.16, f32[40,256]{1,0:T(8,128)} %copy-done.14, f32[256,256]{1,0:T(8,128)S(1)} %fusion.76, pred[256,256]{1,0:T(8,128)(4,1)} %copy-done.12, ...), kind=kOutput, calls=%fused_computation.44 | convolution fusion | flops 2027683840 | bytes 5693600 | tf_op jit(solution)/shard_map/jvp()/while/body/eval_jaxpr/hij,jhp->ihp/dot_general | solution.py:56
  467.4 2.4 copy.41
  469.9 4.2 fusion.57
  474.1 0.6 fusion.94
  474.8 1.7 fusion.25
  (109 shorter events, 2.6 us)
Async XLA Ops:
  7.2 1.3 copy-start
  7.2 136.2 %all-gather.11.cloned.1.call-start = ((), (), s32[]{:S(2)}) async-start(), calls=%async_computation.2 | async-start | bytes 11141120 | tf_op jit(solution)/shard_map/all_gather | solution.py:15
  10.0 298.6 %copy-start.16 = (f32[40,256]{1,0:T(8,128)}, f32[40,256]{1,0:T(8,128)S(1)}, u32[]{:S(2)}) copy-start(f32[40,256]{1,0:T(8,128)S(1)} %get-tuple-element.612) | copy-start | bytes 122884
  14.4 3.1 copy-start.3
  16.7 270.3 %all-gather.7.cloned.1.call-start = ((), (), s32[]{:S(2)}) async-start(), calls=%async_computation | async-start | bytes 13926400 | tf_op jit(solution)/shard_map/all_gather | solution.py:123
  17.4 407.5 %all-gather.9.cloned.1.call-start = ((), (), s32[]{:S(2)}) async-start(), calls=%async_computation.1 | async-start | bytes 11141120 | tf_op jit(solution)/shard_map/all_gather | solution.py:15
  17.6 291.1 %copy-start.14 = (f32[40,256]{1,0:T(8,128)}, f32[40,256]{1,0:T(8,128)S(1)}, u32[]{:S(2)}) copy-start(f32[40,256]{1,0:T(8,128)S(1)} %get-tuple-element.610) | copy-start | bytes 122884
  167.2 131.5 %copy-start.1 = (f32[40,64,128]{2,1,0:T(8,128)}, f32[40,64,128]{2,1,0:T(8,128)S(1)}, u32[]{:S(2)}) copy-start(f32[40,64,128]{2,1,0:T(8,128)S(1)} %get-tuple-element.540) | copy-start | bytes 3932164
  298.7 4.3 copy-start.6
  308.4 9.6 %copy-start.12 = (pred[256,256]{1,0:T(8,128)(4,1)}, pred[256,256]{1,0:T(8,128)(4,1)S(1)}, u32[]{:S(2)}) copy-start(pred[256,256]{1,0:T(8,128)(4,1)S(1)} %iota_compare_fusion) | copy-start | bytes 196612
  308.7 9.8 %copy-start.2 = (f32[40,64,128]{2,1,0:T(8,128)S(1)}, f32[40,64,128]{2,1,0:T(8,128)}, u32[]{:S(2)}) copy-start(f32[40,64,128]{2,1,0:T(8,128)} %copy-done.1) | copy-start | bytes 3932164
  308.7 9.8 %copy-start.7 = (bf16[256,2560]{0,1:T(8,128)(2,1)S(1)}, bf16[256,2560]{0,1:T(8,128)(2,1)}, u32[]{:S(2)}) copy-start(bf16[256,2560]{0,1:T(8,128)(2,1)} %copy.34) | copy-start | bytes 3932164
  308.7 12.4 %copy-start.9 = (f32[256,40,64]{0,2,1:T(8,128)S(1)}, f32[256,40,64]{0,2,1:T(8,128)}, u32[]{:S(2)}) copy-start(f32[256,40,64]{0,2,1:T(8,128)} %get-tuple-element.615) | copy-start | bytes 7864324
  308.7 19.7 %slice-start = ((s8[13107200]{0:T(1024)(128)(4,1)}), s8[4194304]{0:T(1024)(128)(4,1)S(1)}, s32[]{:S(2)}) async-start(s8[13107200]{0:T(1024)(128)(4,1)} %bitcast.210), calls=%async_computation.3 | async-start | bytes 8388608
  308.7 19.7 %slice-start.1 = ((s8[13107200]{0:T(1024)(128)(4,1)}), s8[4194304]{0:T(1024)(128)(4,1)S(1)}, s32[]{:S(2)}) async-start(s8[13107200]{0:T(1024)(128)(4,1)} %bitcast.210), calls=%async_computation.4 | async-start | bytes 8388608
  308.7 19.7 %slice-start.2 = ((s8[13107200]{0:T(1024)(128)(4,1)}), s8[4194304]{0:T(1024)(128)(4,1)S(1)}, s32[]{:S(2)}) async-start(s8[13107200]{0:T(1024)(128)(4,1)} %bitcast.210), calls=%async_computation.5 | async-start | bytes 8388608
  318.0 3.0 copy-start.4
  318.0 3.0 copy-start.15
  318.0 3.1 copy-start.17
  318.0 3.1 copy-start.19
  318.0 3.1 copy-start.13
  321.1 7.3 %slice-start.3 = ((s8[13107200]{0:T(1024)(128)(4,1)}), s8[524288]{0:T(1024)(128)(4,1)S(1)}, s32[]{:S(2)}) async-start(s8[13107200]{0:T(1024)(128)(4,1)} %bitcast.210), calls=%async_computation.6 | async-start | bytes 1048576
  448.2 1.8 copy-start.5
  469.8 4.3 copy-start.11
  469.8 4.3 copy-start.18
  469.9 4.9 %copy-start.8 = (f32[256,2560]{1,0:T(8,128)S(1)}, f32[256,2560]{1,0:T(8,128)}, u32[]{:S(2)}) copy-start(f32[256,2560]{1,0:T(8,128)} %fusion.111) | copy-start | bytes 7864324
  469.9 4.9 %copy-start.10 = (bf16[2560,256]{1,0:T(8,128)(2,1)S(1)}, bf16[2560,256]{1,0:T(8,128)(2,1)}, u32[]{:S(2)}) copy-start(bf16[2560,256]{1,0:T(8,128)(2,1)} %param.14) | copy-start | bytes 3932164
Sparse Core Ops, SparseCore 0:
  16.8 126.5 all-gather.10
  146.1 140.7 all-gather.6
  305.4 119.4 all-gather.8
where the time goes:
time: 486 us; the launch traced here: 483 us
  waiting for transfers between devices  293 us (60%)
  matrix products  66.4 us (14%)
  other arithmetic  56.4 us (12%)
  blocking collectives  43.8 us (9%)
  between operations  14.2 us (3%)
  local copies, waits for them, and re-layouts  7.68 us (2%)
    all_gather x2, waiting for transfers between devices, prefix(): lax.all_gather(part.astype(kind), axis)  173 us
    all_gather x1, waiting for transfers between devices, local(): full_panel = lax.all_gather(w_x, 'dp', axis=1, tiled=True)  120 us
    select_n x32, other arithmetic, lap(): return jax.tree.map(lambda a, b: jnp.where(reached, a, b), new, before)  45.6 us
    all_gather x1, blocking collectives, prefix(): lax.all_gather(part.astype(kind), axis)  43.8 us
    dot_general x3, matrix products, group_forward(): jnp.einsum('hij,jhp->ihp', mixing, x_block, precision=HIGHEST_PRECISION)  27.5 us
  transfers between devices with their start and end apart: 3, of which 3 were waited for; matrix products, arithmetic and copies ran while one was open for 11% of the time, Pallas kernels for 0%

commit v1 on v0

v1 whole, which is shorter than its diff:
```python
import functools

import jax
import jax.numpy as jnp
from jax import lax
from jax.experimental import pallas as pl
from jax.experimental.pallas import tpu as pltpu
from jax.sharding import PartitionSpec as P

MESH = pl.DeviceIdType.MESH
F32 = jnp.float32
BF16 = jnp.bfloat16
HI = lax.Precision.HIGHEST

NN = (((1,), (0,)), ((), ()))
NT = (((1,), (1,)), ((), ()))
TN = (((0,), (0,)), ((), ()))

HEAD = 64
PAIR = 128
PANEL = 160
UNIT = 16
HALF = 80
XUNITS = 15
ZUNITS = 20
STEPS = 28


def mm(a, b, dims=NN):
    return lax.dot_general(a, b, dims, preferred_element_type=F32)


def kernel(
    tok_ref, wt_in, wbc_ref, wdt_ref, par_ref, gy_ref,
    y_ref, dtok_ref,
    wt, x_t, gy_t, xw, gw, gx_t, gx_n, y_t,
    run_s, step_s, sig_s, er_s, tail_s, left_s, a_own, q_s, acc_a, both_s, lam_s,
    bt_s, ct_s, b_s, c_s, st_s, mt_s, dst_s, gbc_s,
    s_loc, g_loc, ent, later, f1, f2, fo, g1, g2, go, tsend, ay, az,
    cp_sem, xs_s, xr_s, zs_s, zr_s, ds_s, dr_s, es_s, er_sem, as_s, ar_s,
):
    dp = lax.axis_index("dp")
    cx = lax.axis_index("ctx")
    x = dp // 4
    zh = (dp // 2) % 2
    c = dp % 2
    zl = cx // 4
    y = cx % 4
    z = zh * 4 + zl
    npair = x_t.shape[0] // PAIR
    own_rows = x_t.shape[0] // 4
    own_heads = own_rows // HEAD
    nhead = run_s.shape[0]

    def at_x(k):
        return (((x + k) % 4) * 4 + zh * 2 + c, cx)

    def at_z(k):
        zz = (z + k + 8) % 8
        return (x * 4 + (zz // 4) * 2 + c, (zz % 4) * 4 + y)

    def at_y(k):
        return (dp, zl * 4 + (y + k) % 4)

    def at_zl(k):
        return (dp, ((zl + k + 4) % 4) * 4 + y)

    sibling = (x * 4 + zh * 2 + (1 - c), cx)

    def remote(src, dst, send, recv, device):
        return pltpu.make_async_remote_copy(
            src_ref=src, dst_ref=dst, send_sem=send, recv_sem=recv,
            device_id=device, device_id_type=MESH,
        )

    def panel_row(xx, half, core):
        return ((xx % 4) * 4 + half * 2 + core) * PANEL

    own = pl.multiple_of(panel_row(x, zh, c), UNIT)
    cp = pltpu.make_async_copy(wt_in, wt.at[pl.ds(own, PANEL)], cp_sem)
    cp.start()

    barrier = pltpu.get_barrier_semaphore()
    peers = [at_x(1), at_x(3), at_z(1), at_z(-1), sibling]
    peers += [at_y(k) for k in (1, 2, 3)] + [at_zl(k) for k in (1, 2, 3)]
    for peer in peers:
        pl.semaphore_signal(barrier, inc=1, device_id=peer, device_id_type=MESH)
    pl.semaphore_wait(barrier, len(peers))
    cp.wait()

    def rows(start, size):
        return wt.at[pl.ds(pl.multiple_of(start, UNIT), size)]

    def x_copy(way, j):
        if way == 0:
            start = jnp.where(
                j < 10, panel_row(x, zh, c) + UNIT * j,
                panel_row(x + 1, zh, c) + UNIT * (j - 10),
            )
            device = at_x(3)
        else:
            start = jnp.where(
                j < 10, panel_row(x, zh, c) + UNIT * ((j + 5) % 10),
                panel_row(x + 3, zh, c) + UNIT * (j - 5),
            )
            device = at_x(1)
        ref = rows(start, UNIT)
        return remote(ref, ref, xs_s.at[way, j], xr_s.at[way, j], device)

    def order(way, g):
        if way == 0:
            return jnp.where(g == 2, 3, jnp.where(g == 3, 2, g))
        return jnp.where(g == 1, 3, jnp.where(g == 2, 1, jnp.where(g == 3, 2, 0)))

    is_source = [zl == 3, zl == 0]

    def z_copy(way, k):
        half = jnp.where(is_source[way], zh, 1 - zh)
        start = panel_row(x + order(way, k // 5), half, c) + UNIT * (k % 5) + HALF * way
        ref = rows(start, UNIT)
        return remote(
            ref, ref, zs_s.at[way, k], zr_s.at[way, k], at_z(1) if way == 0 else at_z(-1)
        )

    def sib_copy(index, start, size):
        ref = rows(start, size)
        return remote(ref, ref, ds_s.at[index], dr_s.at[index], sibling)

    def sib_x(way, t):
        if way == 0:
            start = jnp.where(t == 2, panel_row(x + 2, zh, c), panel_row(x + 1, zh, c) + HALF * (t % 2))
        else:
            start = jnp.where(
                t == 2, panel_row(x + 2, zh, c) + HALF, panel_row(x + 3, zh, c) + HALF * ((t + 1) % 2)
            )
        return sib_copy(2 * t + way, start, HALF)

    def sib_z(way, g):
        start = panel_row(x + order(way, g), 1 - zh, c) + HALF * way
        return sib_copy(6 + 2 * g + way, start, HALF)

    def sib_own():
        ref = rows(own, PANEL)
        return remote(ref, ref, ds_s.at[14], dr_s.at[14], sibling)

    @pl.loop(0, 10)
    def _(j):
        x_copy(0, j).start()
        x_copy(1, j).start()

    for way in (0, 1):
        @pl.when(is_source[way])
        def _():
            @pl.loop(0, 5)
            def _(k):
                z_copy(way, k).start()
    sib_own().start()

    tok = tok_ref[...]
    bc_t = mm(wbc_ref[...], tok, NT)
    nstate = bc_t.shape[0] // 2
    bt_s[...] = bc_t[:nstate].astype(BF16)
    ct_s[...] = bc_t[nstate:].astype(BF16)
    b_s[...] = bc_t[:nstate].T.astype(BF16)
    c_s[...] = bc_t[nstate:].T.astype(BF16)
    raw = mm(wdt_ref[...], tok, NT)[:nhead]
    length = raw.shape[1]
    shifted = raw + par_ref[0]
    step = jnp.maximum(shifted, 0.0) + jnp.log1p(jnp.exp(-jnp.abs(shifted)))
    step_s[...] = step
    sig_s[...] = 1.0 / (1.0 + jnp.exp(-shifted))
    first = lax.broadcasted_iota(jnp.int32, (length, length), 0)
    second = lax.broadcasted_iota(jnp.int32, (length, length), 1)
    upper = jnp.where(first <= second, 1.0, 0.0)
    run = lax.dot_general(-par_ref[1] * step, upper, NN, precision=HI, preferred_element_type=F32)
    run_s[...] = run
    er_s[...] = jnp.exp(run)
    last = run[:, length - 1 :]
    left_s[...] = jnp.exp(last - run)
    tail_s[...] = left_s[...] * step
    a_own[...] = jnp.broadcast_to(jnp.exp(last), a_own.shape)
    st_s[...] = mm(b_s[...], ct_s[...])

    def two(ref, q):
        return jnp.concatenate(
            [jnp.broadcast_to(ref[pl.ds(2 * q + i, 1), :], (HEAD, length)) for i in (0, 1)], axis=0
        )

    def pair_rows(q):
        return pl.ds(pl.multiple_of(q * PAIR, PAIR), PAIR)

    @pl.loop(0, npair)
    def _(q):
        at = pair_rows(q)
        g = gy_ref[:, at].astype(F32).T
        gy_t[at, :] = g.astype(BF16)
        scaled = (g * two(er_s, q)).astype(BF16)
        gw[at, :] = scaled
        g_loc[at, :] = mm(scaled, c_s[...]).astype(BF16)

    def a_y(k):
        return remote(a_own, ay.at[y], as_s.at[k - 1], ar_s.at[k - 1], at_y(k))

    def a_z(k):
        return remote(az.at[zl], az.at[zl], as_s.at[k + 2], ar_s.at[k + 2], at_zl(k))

    for k in (1, 2, 3):
        a_y(k).start()
    ay[y] = a_own[...]

    def my_rows(k):
        return pl.ds(pl.multiple_of(((y + k) % 4) * own_rows, own_rows), own_rows)

    def e_first(src, got, base, k):
        return remote(
            src.at[my_rows(k)], got.at[y], es_s.at[base + k - 1], er_sem.at[base + k - 1], at_y(k)
        )

    def e_total(way, got, base, k):
        device = at_zl(k) if way == 0 else at_zl(-k)
        return remote(
            tsend.at[way], got.at[zl], es_s.at[base + 2 + k], er_sem.at[base + 2 + k], device
        )

    def e_back(out, res, base, k):
        return remote(
            out.at[(y + k) % 4], res.at[my_rows(0)],
            es_s.at[base + 5 + k], er_sem.at[base + 5 + k], at_y(k),
        )

    def begin(src, got, base):
        for k in (1, 2, 3):
            e_first(src, got, base, k).start()
        got[y] = src[my_rows(0), :]

    def head_rows(h):
        return pl.ds(pl.multiple_of(h * HEAD, HEAD), HEAD)

    def decay(ref, slot, h):
        return ref[slot, pl.ds(y * own_heads + h, 1), :]

    def totals(way, src, got1, got2, base):
        for k in (1, 2, 3):
            e_first(src, got1, base, k).wait()
        ys = (0, 1, 2, 3) if way == 0 else (3, 2, 1, 0)

        @pl.loop(0, own_heads)
        def _(h):
            t = got1[ys[0], head_rows(h), :].astype(F32)
            for s in ys[1:]:
                t = decay(ay, s, h) * t + got1[s, head_rows(h), :].astype(F32)
            tsend[way, head_rows(h), :] = t.astype(BF16)

        for k in (1, 2, 3):
            ok = (zl + k < 4) if way == 0 else (zl - k >= 0)

            @pl.when(ok)
            def _():
                e_total(way, got2, base, k).start()

    def spread(way, got1, got2, out, res, base, work):
        for k in (1, 2, 3):
            ok = (zl - k >= 0) if way == 0 else (zl + k < 4)

            @pl.when(ok)
            def _():
                e_total(way, got2, base, k).wait_recv()
        ys = (0, 1, 2, 3) if way == 0 else (3, 2, 1, 0)
        zs = (0, 1, 2) if way == 0 else (3, 2, 1)

        @pl.loop(0, own_heads)
        def _(h):
            work[...] = jnp.zeros_like(work)
            for s in zs:
                @pl.when(s < zl if way == 0 else s > zl)
                def _():
                    work[...] = decay(az, s, h) * work[...] + got2[s, head_rows(h), :].astype(F32)
            e = work[...]
            for s in ys:
                out[s, head_rows(h), :] = e.astype(BF16)
                if s != ys[-1]:
                    e = decay(ay, s, h) * e + got1[s, head_rows(h), :].astype(F32)

        for k in (1, 2, 3):
            e_back(out, res, base, k).start()
        res[my_rows(0), :] = out[y]

    def finish(way, out, res, got2, base):
        for k in (1, 2, 3):
            e_back(out, res, base, k).wait()
            ok = (zl + k < 4) if way == 0 else (zl - k >= 0)

            @pl.when(ok)
            def _():
                e_total(way, got2, base, k).wait_send()

    begin(g_loc, g1, 0)

    for k in (1, 2, 3):
        a_y(k).wait()
    az[zl] = ay[0] * ay[1] * ay[2] * ay[3]
    for k in (1, 2, 3):
        a_z(k).start()

    @pl.loop(0, STEPS)
    def _(s):
        j = s - 2

        @pl.when((j >= 0) & (j < XUNITS))
        def _():
            for way in (0, 1):
                x_copy(way, j).wait_recv()

            @pl.when(j < 5)
            def _():
                for way in (0, 1):
                    x_copy(way, j + 10).start()

            for way in (0, 1):
                @pl.when(is_source[way])
                def _():
                    z_copy(way, j + 5).start()

            @pl.when(j % 5 == 4)
            def _():
                for way in (0, 1):
                    sib_x(way, j // 5).start()

        for way in (0, 1):
            k = s - 2 - 2 * (zl if way == 0 else 3 - zl)

            @pl.when((k >= 0) & (k < ZUNITS))
            def _():
                z_copy(way, k).wait_recv()

                @pl.when(jnp.logical_not(is_source[way]))
                def _():
                    z_copy(way, k).start()

                @pl.when(k % 5 == 4)
                def _():
                    sib_z(way, k // 5).start()

    for k in (1, 2, 3):
        a_z(k).wait()
    totals(1, g_loc, g1, g2, 0)
    spread(1, g1, g2, go, later, 0, lam_s)

    sib_own().wait()
    for t in range(3):
        for way in (0, 1):
            sib_x(way, t).wait()
    for g in range(4):
        for way in (0, 1):
            sib_z(way, g).wait()

    @pl.loop(0, XUNITS)
    def _(j):
        for way in (0, 1):
            x_copy(way, j).wait_send()

    @pl.loop(0, ZUNITS)
    def _(k):
        for way in (0, 1):
            z_copy(way, k).wait_send()

    @pl.loop(0, 4)
    def _(g):
        at = pl.ds(pl.multiple_of(g * own_rows, own_rows), own_rows)
        x_t[at, :] = mm(wt[at, :], tok_ref[...], NT).astype(BF16)

    @pl.loop(0, npair)
    def _(q):
        at = pair_rows(q)
        scaled = (x_t[at, :].astype(F32) * two(tail_s, q)).astype(BF16)
        xw[at, :] = scaled
        s_loc[at, :] = mm(scaled, b_s[...]).astype(BF16)

    begin(s_loc, f1, 9)
    totals(0, s_loc, f1, f2, 9)
    finish(1, go, later, g2, 0)

    dst_s[...] = jnp.zeros_like(dst_s)
    mt_s[...] = jnp.zeros_like(mt_s)
    side = length // 2
    keep = (
        lax.broadcasted_iota(jnp.int32, (side, side), 0)
        <= lax.broadcasted_iota(jnp.int32, (side, side), 1)
    )

    @pl.loop(0, nhead)
    def _(h):
        at = head_rows(h)
        r = run_s[pl.ds(h, 1), :]
        r_col = jnp.broadcast_to(r, (side, length)).T
        e00 = jnp.exp(jnp.where(keep, r[:, :side] - r_col[:side], -1e30))
        e01 = jnp.exp(r[:, side:] - r_col[:side])
        e11 = jnp.exp(jnp.where(keep, r[:, side:] - r_col[side:], -1e30))
        mt_s[:side, :side] = (e00 * st_s[:side, :side]).astype(BF16)
        mt_s[:side, side:] = (e01 * st_s[:side, side:]).astype(BF16)
        mt_s[side:, side:] = (e11 * st_s[side:, side:]).astype(BF16)
        xs = (x_t[at, :].astype(F32) * step_s[pl.ds(h, 1), :]).astype(BF16)
        gy = gy_t[at, :]
        y_t[at, :] = mm(xs, mt_s[...])
        gx_t[at, :] = mm(gy, mt_s[...], NT)
        pull = mm(xs, gy, TN)
        dst_s[:side, :side] += pull[:side, :side] * e00
        dst_s[:side, side:] += pull[:side, side:] * e01
        dst_s[side:, side:] += pull[side:, side:] * e11

    @pl.loop(0, npair)
    def _(q):
        at = pair_rows(q)
        g = gx_t[at, :] + two(left_s, q) * mm(later[at, :], bt_s[...])
        prod = x_t[at, :].astype(F32) * g
        for i in (0, 1):
            q_s[pl.ds(2 * q + i, 1), :] = jnp.sum(
                prod[i * HEAD : (i + 1) * HEAD], axis=0, keepdims=True
            )
        g = g * two(step_s, q) + two(par_ref.at[2], q) * gy_t[at, :].astype(F32)
        gx_n[:, at] = g.T.astype(BF16)

    spread(0, f1, f2, fo, ent, 9, lam_s)
    finish(0, fo, ent, f2, 9)

    @pl.loop(0, npair)
    def _(q):
        at = pair_rows(q)
        inner = y_t[at, :] + two(er_s, q) * mm(ent[at, :], ct_s[...])
        prod = inner * gy_t[at, :].astype(F32)
        full = inner + two(par_ref.at[2], q) * x_t[at, :].astype(F32)
        y_ref[:, at] = full.T.astype(BF16)
        for i in (0, 1):
            acc_a[pl.ds(2 * q + i, 1), :] = jnp.sum(
                prod[i * HEAD : (i + 1) * HEAD], axis=0, keepdims=True
            )
            hr = pl.ds(pl.multiple_of(q * PAIR + i * HEAD, HEAD), HEAD)
            final = a_own[pl.ds(2 * q + i, 1), :] * ent[hr, :].astype(F32) + s_loc[hr, :].astype(F32)
            both = jnp.sum(later[hr, :].astype(F32) * final, axis=0, keepdims=True)
            both_s[pl.ds(2 * q + i, 1), :] = jnp.broadcast_to(
                jnp.sum(both, axis=1, keepdims=True), (1, length)
            )

    dst = dst_s[...].astype(BF16)
    gb_t = mm(ct_s[...], dst, NT) + mm(later[...], xw[...], TN)
    gc_t = mm(bt_s[...], dst) + mm(ent[...], gw[...], TN)
    gbc_s[:, :nstate] = gb_t.T.astype(BF16)
    gbc_s[:, nstate:] = gc_t.T.astype(BF16)
    lower = jnp.where(first >= second, 1.0, 0.0)
    q_all = q_s[...]
    d_log = lax.dot_general(
        acc_a[...] - step_s[...] * q_all, lower, NN, precision=HI, preferred_element_type=F32
    ) + both_s[...]
    g_raw = ((q_all - par_ref[1] * d_log) * sig_s[...]).astype(BF16)

    wide = 512

    @pl.loop(0, dtok_ref.shape[1] // wide)
    def _(n):
        at = pl.ds(pl.multiple_of(n * wide, wide), wide)
        total = mm(gx_n[...], wt[:, at]) + mm(gbc_s[...], wbc_ref[:, at])
        total = total + mm(g_raw, wdt_ref[:nhead, at], TN)
        dtok_ref[:, at] = total.astype(BF16)


def local(tokens, w_x, w_bc, w_dt, dt_bias, decay_rate, skip_gain, grad_y):
    length, width = tokens.shape[1:]
    hp = grad_y.shape[2]
    heads = dt_bias.shape[0]
    state = w_bc.shape[1] // 2
    own = hp // 4
    params = jnp.broadcast_to(
        jnp.stack([dt_bias, decay_rate, skip_gain])[:, :, None], (3, heads, length)
    )
    vmem = pl.BlockSpec(memory_space=pltpu.VMEM)
    flat = pltpu.VMEM((hp, length), BF16)
    wide = pltpu.VMEM((hp, length), F32)
    per_head = pltpu.VMEM((heads, length), F32)
    states = pltpu.VMEM((hp, state), BF16)
    slots = pltpu.VMEM((4, own, state), BF16)
    decays = pltpu.VMEM((heads, state), F32)
    dma = pltpu.SemaphoreType.DMA
    y, dtok = pl.pallas_call(
        kernel,
        out_shape=(
            jax.ShapeDtypeStruct((length, hp), BF16),
            jax.ShapeDtypeStruct((length, width), BF16),
        ),
        in_specs=[vmem] * 6,
        out_specs=(vmem, vmem),
        scratch_shapes=[
            pltpu.VMEM((hp, width), BF16), flat, flat, flat, flat, wide,
            pltpu.VMEM((length, hp), BF16), wide,
            per_head, per_head, per_head, per_head, per_head, per_head, decays,
            per_head, per_head, per_head,
            pltpu.VMEM((HEAD, state), F32),
            pltpu.VMEM((state, length), BF16), pltpu.VMEM((state, length), BF16),
            pltpu.VMEM((length, state), BF16), pltpu.VMEM((length, state), BF16),
            pltpu.VMEM((length, length), F32), pltpu.VMEM((length, length), BF16),
            pltpu.VMEM((length, length), F32), pltpu.VMEM((length, 2 * state), BF16),
            states, states, states, states, slots, slots, slots, slots, slots, slots,
            pltpu.VMEM((2, own, state), BF16),
            pltpu.VMEM((4, heads, state), F32), pltpu.VMEM((4, heads, state), F32),
            dma, dma((2, XUNITS)), dma((2, XUNITS)), dma((2, ZUNITS)), dma((2, ZUNITS)),
            dma((15,)), dma((15,)), dma((18,)), dma((18,)), dma((6,)), dma((6,)),
        ],
        compiler_params=pltpu.CompilerParams(
            collective_id=0, has_side_effects=True, vmem_limit_bytes=60 << 20
        ),
    )(tokens[0], w_x.T, w_bc.T, w_dt.T, params, grad_y[0])
    return (y[None], dtok[None])


def solution(mesh):
    placed = (P("dp", "ctx", None), P(None, "dp"), P(), P(), P(), P(), P(), P("dp", "ctx", None))
    return jax.shard_map(
        local,
        mesh=mesh,
        in_specs=placed,
        out_specs=(P("dp", "ctx", None), P("dp", "ctx", None)),
        check_vma=False,
    )
```

time: 486 us -> 141 us (0.29)
  waiting for transfers between devices: 293 us -> 0 us
  Pallas kernels: 0 us -> 133 us
  matrix products: 66.4 us -> 0 us
  other arithmetic: 56.4 us -> 0.7 us
  blocking collectives: 43.8 us -> 0 us
  between operations: 14.2 us -> 0.65 us
    all_gather x3 -> x0, waiting for transfers between devices: 293 us -> none  [the longest x2 173 us: prefix(): lax.all_gather(part.astype(kind), axis)]
    pallas_call x0 -> x1, Pallas kernels: none -> 133 us  [local(): pl.pallas_call(kernel, out_shape=(jax.ShapeDtypeStruct((length, hp), BF16...]
    dot_general x18 -> x0, matrix products: 66.4 us -> none  [the longest x3 27.5 us: group_forward(): jnp.einsum('hij,jhp->ihp', mixing, x_block, precision=HIGHEST_PRECISION)]
    select_n x33 -> x0, other arithmetic: 45.7 us -> none  [the longest x32 45.6 us: lap(): return jax.tree.map(lambda a, b: jnp.where(reached, a, b), new, before)]
    all_gather x1 -> x0, blocking collectives: 43.8 us -> none  [prefix(): lax.all_gather(part.astype(kind), axis)]
  transfers between devices with their start and end apart: 3 -> 0, of which waited for: 3 -> 0; matrix products, arithmetic and copies ran while one was open for 11% -> 0% of each run, Pallas kernels for 0% -> 0%
where the time goes in v1:
time: 141 us
  Pallas kernels  133 us (94%)
  local copies, waits for them, and re-layouts  6.77 us (5%)
    pallas_call x1, Pallas kernels, local(): pl.pallas_call(kernel, out_shape=(jax.ShapeDtypeStruct((length, hp), BF16...  133 us
    unnamed x5, local copies, waits for them, and re-layouts  6.04 us

profile of v1, /device:TPU:2, one launch (start us, length us, event | category | flops | bytes accessed | tf_op | source)
XLA Modules:
  0.0 141.2 jit_solution(2650821274742949462)
XLA Ops:
  0.6 0.7 pad_maximum_fusion
  1.3 0.7 broadcast_in_dim.12.par_ref
  2.1 2.4 %copy.10 = bf16[2560,256]{0,1:T(8,128)(2,1)} copy(bf16[2560,256]{1,0:T(8,128)(2,1)} %param.10) | data formatting | bytes 2621440 | tf_op args[2]
  4.5 133.1 %shard_map.95 = (bf16[256,2560]{1,0:T(8,128)(2,1)}, bf16[256,2560]{1,0:T(8,128)(2,1)}) custom-call(bf16[256,2560]{1,0:T(8,128)(2,1)} %bitcast.13, bf16[160,2560]{1,0:T(8,128)(2,1)} %bitcast.15, bf16[256,2560]{1,0:T(8,128)(2,1)} %bitcast.10, bf16[40,2560]{1,0:T(8,128)(2,1)} %bitcast.16, f32[3,40,256]{2,1,0:T(8,128)} %broadcast_in_dim.12.par_ref, ...), custom_call_target="tpu_custom_call" | custom-call | tf_op jit(solution)/shard_map/pallas_call | solution.py:483
  137.6 0.0 copy-start
  137.6 2.6 %copy.13 = bf16[1,256,2560]{2,1,0:T(8,128)(2,1)} copy(bf16[1,256,2560]{2,1,0:T(8,128)(2,1)} %bitcast.12) | data formatting | bytes 2621440
  140.1 0.0 copy-done
  140.1 1.1 copy.14
Async XLA Ops:
  137.6 2.6 %copy-start = (bf16[256,2560]{1,0:T(8,128)(2,1)S(1)}, bf16[256,2560]{1,0:T(8,128)(2,1)}, u32[]{:S(2)}) copy-start(bf16[256,2560]{1,0:T(8,128)(2,1)} %get-tuple-element.5) | copy-start | bytes 3932164

commit v2 on v1

v2 whole, which is shorter than its diff:
```python
import functools

import jax
import jax.numpy as jnp
from jax import lax
from jax.experimental import pallas as pl
from jax.experimental.pallas import tpu as pltpu
from jax.sharding import PartitionSpec as P

MESH = pl.DeviceIdType.MESH
F32 = jnp.float32
BF16 = jnp.bfloat16
HI = lax.Precision.HIGHEST

NN = (((1,), (0,)), ((), ()))
NT = (((1,), (1,)), ((), ()))
TN = (((0,), (0,)), ((), ()))

HEAD = 64
PAIR = 128
PANEL = 160
UNIT = 16
HALF = 80
XUNITS = 15
ZUNITS = 20
STEPS = 41
GATHER = 28
ENTER = (12, 22, 23, 28)
LEAVE = (24, 35, 36, 40)
BLOCK = 32
DTOK_FROM = 30


def mm(a, b, dims=NN):
    return lax.dot_general(a, b, dims, preferred_element_type=F32)


def kernel(
    tok_ref, wt_in, wbc_ref, wdt_ref, par_ref, gy_ref,
    y_ref, dtok_ref,
    wt, x_t, gy_t, xw, gw, gx_t, gx_n, y_t, acc_d, e_all, m_all,
    run_s, step_s, sig_s, er_s, tail_s, left_s, a_own, q_s, acc_a, both_s,
    bt_s, ct_s, b_s, c_s, st_s, dst_s, gbc_s,
    s_loc, g_loc, ent, later, first_f, total_f, enter_f, pass_f, out_f,
    first_b, total_b, enter_b, pass_b, out_b, ay,
    cp_sem, xs_s, xr_s, zs_s, zr_s, ds_s, dr_s, es_s, er_sem, as_s, ar_s,
):
    dp = lax.axis_index("dp")
    cx = lax.axis_index("ctx")
    x = dp // 4
    zh = (dp // 2) % 2
    c = dp % 2
    zl = cx // 4
    y = cx % 4
    z = zh * 4 + zl
    group = x_t.shape[0] // 4
    group_heads = group // HEAD
    group_pairs = group // PAIR
    slice_rows = group // 4
    nhead = run_s.shape[0]

    def at_x(k):
        return (((x + k) % 4) * 4 + zh * 2 + c, cx)

    def at_z(k):
        zz = (z + k + 8) % 8
        return (x * 4 + (zz // 4) * 2 + c, (zz % 4) * 4 + y)

    def at_y(k):
        return (dp, zl * 4 + (y + k) % 4)

    sibling = (x * 4 + zh * 2 + (1 - c), cx)

    def remote(src, dst, send, recv, device):
        return pltpu.make_async_remote_copy(
            src_ref=src, dst_ref=dst, send_sem=send, recv_sem=recv,
            device_id=device, device_id_type=MESH,
        )

    def panel_row(xx, half, core):
        return ((xx % 4) * 4 + half * 2 + core) * PANEL

    own = pl.multiple_of(panel_row(x, zh, c), UNIT)
    cp = pltpu.make_async_copy(wt_in, wt.at[pl.ds(own, PANEL)], cp_sem)
    cp.start()

    barrier = pltpu.get_barrier_semaphore()
    peers = [at_x(1), at_x(3), at_z(1), at_z(-1), sibling]
    peers += [at_y(k) for k in (1, 2, 3)]
    for peer in peers:
        pl.semaphore_signal(barrier, inc=1, device_id=peer, device_id_type=MESH)
    pl.semaphore_wait(barrier, len(peers))
    cp.wait()

    def rows(start, size):
        return wt.at[pl.ds(pl.multiple_of(start, UNIT), size)]

    def x_copy(way, j):
        if way == 0:
            start = jnp.where(
                j < 10, panel_row(x, zh, c) + UNIT * j,
                panel_row(x + 1, zh, c) + UNIT * (j - 10),
            )
            device = at_x(3)
        else:
            start = jnp.where(
                j < 10, panel_row(x, zh, c) + UNIT * ((j + 5) % 10),
                panel_row(x + 3, zh, c) + UNIT * (j - 5),
            )
            device = at_x(1)
        ref = rows(start, UNIT)
        return remote(ref, ref, xs_s.at[way, j], xr_s.at[way, j], device)

    def order(way, g):
        if way == 0:
            return jnp.where(g == 2, 3, jnp.where(g == 3, 2, g))
        return jnp.where(g == 1, 3, jnp.where(g == 2, 1, jnp.where(g == 3, 2, 0)))

    is_source = [zl == 3, zl == 0]

    def z_copy(way, k):
        half = jnp.where(is_source[way], zh, 1 - zh)
        start = panel_row(x + order(way, k // 5), half, c) + UNIT * (k % 5) + HALF * way
        ref = rows(start, UNIT)
        return remote(
            ref, ref, zs_s.at[way, k], zr_s.at[way, k], at_z(1) if way == 0 else at_z(-1)
        )

    def sib_copy(index, start, size):
        ref = rows(start, size)
        return remote(ref, ref, ds_s.at[index], dr_s.at[index], sibling)

    def sib_x(way, t):
        if way == 0:
            start = jnp.where(t == 2, panel_row(x + 2, zh, c), panel_row(x + 1, zh, c) + HALF * (t % 2))
        else:
            start = jnp.where(
                t == 2, panel_row(x + 2, zh, c) + HALF, panel_row(x + 3, zh, c) + HALF * ((t + 1) % 2)
            )
        return sib_copy(2 * t + way, start, HALF)

    def sib_z(way, g):
        start = panel_row(x + order(way, g), 1 - zh, c) + HALF * way
        return sib_copy(6 + 2 * g + way, start, HALF)

    def sib_own():
        ref = rows(own, PANEL)
        return remote(ref, ref, ds_s.at[14], dr_s.at[14], sibling)

    @pl.loop(0, 10)
    def _(j):
        x_copy(0, j).start()
        x_copy(1, j).start()

    for way in (0, 1):
        @pl.when(is_source[way])
        def _():
            @pl.loop(0, 5)
            def _(k):
                z_copy(way, k).start()
    sib_own().start()

    tok = tok_ref[...]
    bc_t = mm(wbc_ref[...], tok, NT)
    nstate = bc_t.shape[0] // 2
    bt_s[...] = bc_t[:nstate].astype(BF16)
    ct_s[...] = bc_t[nstate:].astype(BF16)
    b_s[...] = bc_t[:nstate].T.astype(BF16)
    c_s[...] = bc_t[nstate:].T.astype(BF16)
    raw = mm(wdt_ref[...], tok, NT)[:nhead]
    length = raw.shape[1]
    shifted = raw + par_ref[0]
    step = jnp.maximum(shifted, 0.0) + jnp.log1p(jnp.exp(-jnp.abs(shifted)))
    step_s[...] = step
    sig_s[...] = 1.0 / (1.0 + jnp.exp(-shifted))
    first = lax.broadcasted_iota(jnp.int32, (length, length), 0)
    second = lax.broadcasted_iota(jnp.int32, (length, length), 1)
    upper = jnp.where(first <= second, 1.0, 0.0)
    run = lax.dot_general(-par_ref[1] * step, upper, NN, precision=HI, preferred_element_type=F32)
    run_s[...] = run
    er_s[...] = jnp.exp(run)
    last = run[:, length - 1 :]
    left_s[...] = jnp.exp(last - run)
    tail_s[...] = left_s[...] * step
    a_own[...] = jnp.broadcast_to(jnp.exp(last), a_own.shape)
    st_s[...] = mm(b_s[...], ct_s[...])

    def two(ref, q):
        return jnp.concatenate(
            [jnp.broadcast_to(ref[pl.ds(2 * q + i, 1), :], (HEAD, length)) for i in (0, 1)], axis=0
        )

    def pair_rows(q):
        return pl.ds(pl.multiple_of(q * PAIR, PAIR), PAIR)

    def a_y(k):
        return remote(a_own, ay.at[y], as_s.at[k - 1], ar_s.at[k - 1], at_y(k))

    for k in (1, 2, 3):
        a_y(k).start()
    ay[y] = a_own[...]

    def head_rows(h):
        return pl.ds(pl.multiple_of(h * HEAD, HEAD), HEAD)

    def group_base(way, g):
        return ((x + order(0, g)) % 4 if way == 0 else g) * group

    src_of = (s_loc, g_loc)
    first_of = (first_f, first_b)
    total_of = (total_f, total_b)
    enter_of = (enter_f, enter_b)
    pass_of = (pass_f, pass_b)
    out_of = (out_f, out_b)
    res_of = (ent, later)
    ys_of = ((0, 1, 2, 3), (3, 2, 1, 0))
    starts = (zl == 0, zl == 3)
    ends = (zl == 3, zl == 0)

    def slice_at(way, g, k):
        start = group_base(way, g) + ((y + k) % 4) * slice_rows
        return pl.ds(pl.multiple_of(start, UNIT), slice_rows)

    def e_first(way, g, k):
        return remote(
            src_of[way].at[slice_at(way, g, k)], first_of[way].at[g, y],
            es_s.at[way, g, k - 1], er_sem.at[way, g, k - 1], at_y(k),
        )

    def e_pass(way, g):
        return remote(
            pass_of[way].at[g], enter_of[way].at[g], es_s.at[way, g, 3], er_sem.at[way, g, 3],
            at_z(1) if way == 0 else at_z(-1),
        )

    def e_back(way, g, k):
        return remote(
            out_of[way].at[g, (y + k) % 4], res_of[way].at[slice_at(way, g, 0)],
            es_s.at[way, g, 3 + k], er_sem.at[way, g, 3 + k], at_y(k),
        )

    def begin(way, g):
        for k in (1, 2, 3):
            e_first(way, g, k).start()
        first_of[way][g, y] = src_of[way][slice_at(way, g, 0), :]

    def block_rows(b):
        return pl.ds(pl.multiple_of(b * BLOCK, BLOCK), BLOCK)

    def block_decay(way, g, b):
        h = group_base(way, g) // HEAD + (y * slice_rows + b * BLOCK) // HEAD
        return [ay[s, pl.ds(h, 1), :] for s in range(4)]

    def totals(way, g):
        for k in (1, 2, 3):
            e_first(way, g, k).wait_recv()

        @pl.loop(0, slice_rows // BLOCK)
        def _(b):
            at = block_rows(b)
            d = block_decay(way, g, b)
            ys = ys_of[way]
            t = first_of[way][g, ys[0], at, :].astype(F32)
            for s in ys[1:]:
                t = d[s] * t + first_of[way][g, s, at, :].astype(F32)
            total_of[way][g, at, :] = t
            pass_of[way][g, at, :] = t.astype(BF16)

        @pl.when(starts[way])
        def _():
            e_pass(way, g).start()
            enter_of[way][g] = jnp.zeros(enter_of[way].shape[1:], BF16)

    def chain(way, g):
        @pl.when(jnp.logical_not(starts[way]))
        def _():
            e_pass(way, g).wait_recv()

            @pl.when(jnp.logical_not(ends[way]))
            def _():
                @pl.loop(0, slice_rows // BLOCK)
                def _(b):
                    at = block_rows(b)
                    d = block_decay(way, g, b)
                    e = enter_of[way][g, at, :].astype(F32)
                    e = d[0] * d[1] * d[2] * d[3] * e + total_of[way][g, at, :]
                    pass_of[way][g, at, :] = e.astype(BF16)

                e_pass(way, g).start()

        @pl.loop(0, slice_rows // BLOCK)
        def _(b):
            at = block_rows(b)
            d = block_decay(way, g, b)
            ys = ys_of[way]
            e = enter_of[way][g, at, :].astype(F32)
            for s in ys:
                out_of[way][g, s, at, :] = e.astype(BF16)
                if s != ys[-1]:
                    e = d[s] * e + first_of[way][g, s, at, :].astype(F32)

        for k in (1, 2, 3):
            e_back(way, g, k).start()
        res_of[way][slice_at(way, g, 0), :] = out_of[way][g, y]

    def finish(way, g):
        for k in (1, 2, 3):
            e_back(way, g, k).wait_recv()

    def drain(way, g):
        for k in (1, 2, 3):
            e_first(way, g, k).wait_send()
            e_back(way, g, k).wait_send()

        @pl.when(jnp.logical_not(ends[way]))
        def _():
            e_pass(way, g).wait_send()

    side = length // 2
    keep = (
        lax.broadcasted_iota(jnp.int32, (side, side), 0)
        <= lax.broadcasted_iota(jnp.int32, (side, side), 1)
    )
    dst_s[...] = jnp.zeros_like(dst_s)

    def own_states(q):
        at = pair_rows(q)
        g = gy_ref[:, at].astype(F32).T
        gy_t[at, :] = g.astype(BF16)
        scaled = (g * two(er_s, q)).astype(BF16)
        gw[at, :] = scaled
        g_loc[at, :] = mm(scaled, c_s[...]).astype(BF16)

    def mixing(h):
        at = head_rows(h)
        r = run_s[pl.ds(h, 1), :]
        r_col = jnp.broadcast_to(r, (side, length)).T
        e00 = jnp.exp(jnp.where(keep, r[:, :side] - r_col[:side], -1e30))
        e01 = jnp.exp(r[:, side:] - r_col[:side])
        e11 = jnp.exp(jnp.where(keep, r[:, side:] - r_col[side:], -1e30))
        e_all[h, :side, :side] = e00.astype(BF16)
        e_all[h, :side, side:] = e01.astype(BF16)
        e_all[h, side:, side:] = e11.astype(BF16)
        m_all[h, :side, :side] = (e00 * st_s[:side, :side]).astype(BF16)
        m_all[h, :side, side:] = (e01 * st_s[:side, side:]).astype(BF16)
        m_all[h, side:, :side] = jnp.zeros((side, side), BF16)
        m_all[h, side:, side:] = (e11 * st_s[side:, side:]).astype(BF16)
        gx_t[at, :] = mm(gy_t[at, :], m_all[h], NT)

    def pull_back(q):
        at = pair_rows(q)
        g = gx_t[at, :] + two(left_s, q) * mm(later[at, :], bt_s[...])
        gx_t[at, :] = g
        g = g * two(step_s, q) + two(par_ref.at[2], q) * gy_t[at, :].astype(F32)
        gx_n[:, at] = g.T.astype(BF16)

    def project(g):
        base = group_base(0, g)
        at = pl.ds(pl.multiple_of(base, group), group)
        x_t[at, :] = mm(wt[at, :], tok_ref[...], NT).astype(BF16)

        @pl.loop(0, group_pairs)
        def _(i):
            q = base // PAIR + i
            here = pair_rows(q)
            scaled = (x_t[here, :].astype(F32) * two(tail_s, q)).astype(BF16)
            xw[here, :] = scaled
            s_loc[here, :] = mm(scaled, b_s[...]).astype(BF16)

    def inside(h):
        at = head_rows(h)
        xh = x_t[at, :].astype(F32)
        xs = (xh * step_s[pl.ds(h, 1), :]).astype(BF16)
        gy = gy_t[at, :]
        y_t[at, :] = mm(xs, m_all[h])
        pull = mm(xs, gy, TN)
        dst_s[:side, :side] += pull[:side, :side] * e_all[h, :side, :side].astype(F32)
        dst_s[:side, side:] += pull[:side, side:] * e_all[h, :side, side:].astype(F32)
        dst_s[side:, side:] += pull[side:, side:] * e_all[h, side:, side:].astype(F32)

    def outputs(q):
        at = pair_rows(q)
        xq = x_t[at, :].astype(F32)
        inner = y_t[at, :] + two(er_s, q) * mm(ent[at, :], ct_s[...])
        prod = inner * gy_t[at, :].astype(F32)
        back = xq * gx_t[at, :]
        full = inner + two(par_ref.at[2], q) * xq
        y_ref[:, at] = full.T.astype(BF16)
        for i in (0, 1):
            part = slice(i * HEAD, (i + 1) * HEAD)
            acc_a[pl.ds(2 * q + i, 1), :] = jnp.sum(prod[part], axis=0, keepdims=True)
            q_s[pl.ds(2 * q + i, 1), :] = jnp.sum(back[part], axis=0, keepdims=True)
            hr = head_rows(2 * q + i)
            final = a_own[pl.ds(2 * q + i, 1), :] * ent[hr, :].astype(F32) + s_loc[hr, :].astype(F32)
            both = jnp.sum(later[hr, :].astype(F32) * final, axis=0, keepdims=True)
            both_s[pl.ds(2 * q + i, 1), :] = jnp.broadcast_to(
                jnp.sum(both, axis=1, keepdims=True), (1, length)
            )

    wide = dtok_ref.shape[1] // 5

    def columns(n):
        return pl.ds(pl.multiple_of(n * wide, 128), wide)

    def pick(s, table):
        found = -1
        for i, t in enumerate(table):
            found = jnp.where(s == t, i, found)
        return found

    @pl.loop(0, STEPS)
    def _(s):
        j = s - 2

        @pl.when((j >= 0) & (j < XUNITS))
        def _():
            for way in (0, 1):
                x_copy(way, j).wait_recv()

            @pl.when(j < 5)
            def _():
                for way in (0, 1):
                    x_copy(way, j + 10).start()

            for way in (0, 1):
                @pl.when(is_source[way])
                def _():
                    z_copy(way, j + 5).start()

            @pl.when(j % 5 == 4)
            def _():
                for way in (0, 1):
                    sib_x(way, j // 5).start()

        for way in (0, 1):
            k = s - 2 - 2 * (zl if way == 0 else 3 - zl)

            @pl.when((k >= 0) & (k < ZUNITS))
            def _():
                z_copy(way, k).wait_recv()

                @pl.when(jnp.logical_not(is_source[way]))
                def _():
                    z_copy(way, k).start()

                @pl.when(k % 5 == 4)
                def _():
                    sib_z(way, k // 5).start()

        @pl.when(s == 2)
        def _():
            for k in (1, 2, 3):
                a_y(k).wait()

        b = s - 3

        @pl.when((b >= 0) & (b < 4))
        def _():
            totals(1, b)

        b = s - 4 - 2 * (3 - zl)

        @pl.when((b >= 0) & (b < 4))
        def _():
            chain(1, b)

        g_total = pick(s - 2, ENTER)

        @pl.when(g_total >= 0)
        def _():
            totals(0, g_total)

        g_chain = pick(s - 3 - 2 * zl, ENTER)

        @pl.when(g_chain >= 0)
        def _():
            chain(0, g_chain)

        g_enter = pick(s, ENTER)

        @pl.when(g_enter >= 0)
        def _():
            @pl.when(g_enter == 0)
            def _():
                sib_own().wait_recv()

            @pl.when(g_enter > 0)
            def _():
                sib_copy(jnp.where(g_enter == 3, 4, g_enter - 1), 0, HALF).wait_recv()
                sib_copy(jnp.where(g_enter == 3, 5, g_enter + 1), 0, HALF).wait_recv()

            swapped = jnp.where(g_enter == 1, 2, jnp.where(g_enter == 2, 1, g_enter))
            sib_copy(6 + 2 * g_enter, 0, HALF).wait_recv()
            sib_copy(7 + 2 * swapped, 0, HALF).wait_recv()
            project(g_enter)
            begin(0, g_enter)

        @pl.when(s < 4)
        def _():
            @pl.loop(0, group_pairs)
            def _(i):
                own_states(s * group_pairs + i)

            begin(1, s)

        @pl.when((s >= 4) & (s < 14))
        def _():
            @pl.loop(0, 4)
            def _(i):
                mixing((s - 4) * 4 + i)

        b = s - 13

        @pl.when((b >= 0) & (b < 4))
        def _():
            finish(1, b)

            @pl.loop(0, group_pairs)
            def _(i):
                pull_back(b * group_pairs + i)

        def inside_some(first_step, g0, count):
            per = group_heads * count // 5
            n = s - first_step

            @pl.when((n >= 0) & (n < 5))
            def _():
                @pl.loop(0, per)
                def _(i):
                    e = n * per + i
                    g = g0 + e // group_heads
                    inside(group_base(0, g) // HEAD + e % group_heads)

        inside_some(17, 0, 1)
        inside_some(24, 1, 2)
        inside_some(29, 3, 1)

        n = s - DTOK_FROM

        @pl.when((n >= 0) & (n < 5))
        def _():
            acc_d[:, columns(n)] = mm(gx_n[...], wt[:, columns(n)])

        g_leave = pick(s, LEAVE)

        @pl.when(g_leave >= 0)
        def _():
            finish(0, g_leave)

            @pl.loop(0, group_pairs)
            def _(i):
                outputs(group_base(0, g_leave) // PAIR + i)

    dst = dst_s[...].astype(BF16)
    gb_t = mm(ct_s[...], dst, NT) + mm(later[...], xw[...], TN)
    gc_t = mm(bt_s[...], dst) + mm(ent[...], gw[...], TN)
    gbc_s[:, :nstate] = gb_t.T.astype(BF16)
    gbc_s[:, nstate:] = gc_t.T.astype(BF16)
    lower = jnp.where(first >= second, 1.0, 0.0)
    q_all = q_s[...]
    d_log = lax.dot_general(
        acc_a[...] - step_s[...] * q_all, lower, NN, precision=HI, preferred_element_type=F32
    ) + both_s[...]
    g_raw = ((q_all - par_ref[1] * d_log) * sig_s[...]).astype(BF16)

    @pl.loop(0, 5)
    def _(n):
        at = columns(n)
        total = acc_d[:, at] + mm(gbc_s[...], wbc_ref[:, at])
        total = total + mm(g_raw, wdt_ref[:nhead, at], TN)
        dtok_ref[:, at] = total.astype(BF16)

    sib_own().wait_send()
    for t in range(3):
        for way in (0, 1):
            sib_x(way, t).wait_send()
    for g in range(4):
        for way in (0, 1):
            sib_z(way, g).wait_send()

    @pl.loop(0, XUNITS)
    def _(j):
        for way in (0, 1):
            x_copy(way, j).wait_send()

    @pl.loop(0, ZUNITS)
    def _(k):
        for way in (0, 1):
            z_copy(way, k).wait_send()

    @pl.loop(0, 4)
    def _(g):
        for way in (0, 1):
            drain(way, g)


def local(tokens, w_x, w_bc, w_dt, dt_bias, decay_rate, skip_gain, grad_y):
    length, width = tokens.shape[1:]
    hp = grad_y.shape[2]
    heads = dt_bias.shape[0]
    state = w_bc.shape[1] // 2
    piece = hp // 16
    params = jnp.broadcast_to(
        jnp.stack([dt_bias, decay_rate, skip_gain])[:, :, None], (3, heads, length)
    )
    vmem = pl.BlockSpec(memory_space=pltpu.VMEM)
    flat = pltpu.VMEM((hp, length), BF16)
    wide = pltpu.VMEM((hp, length), F32)
    per_head = pltpu.VMEM((heads, length), F32)
    states = pltpu.VMEM((hp, state), BF16)
    slots = pltpu.VMEM((4, 4, piece, state), BF16)
    single = pltpu.VMEM((4, piece, state), BF16)
    exact = pltpu.VMEM((4, piece, state), F32)
    exchange = [slots, exact, single, single, slots]
    decays = pltpu.VMEM((heads, state), F32)
    dma = pltpu.SemaphoreType.DMA
    y, dtok = pl.pallas_call(
        kernel,
        out_shape=(
            jax.ShapeDtypeStruct((length, hp), BF16),
            jax.ShapeDtypeStruct((length, width), BF16),
        ),
        in_specs=[vmem] * 6,
        out_specs=(vmem, vmem),
        scratch_shapes=[
            pltpu.VMEM((hp, width), BF16), flat, flat, flat, flat, wide,
            pltpu.VMEM((length, hp), BF16), wide, pltpu.VMEM((length, width), F32),
            pltpu.VMEM((heads, length, length), BF16), pltpu.VMEM((heads, length, length), BF16),
            per_head, per_head, per_head, per_head, per_head, per_head, decays,
            per_head, per_head, per_head,
            pltpu.VMEM((state, length), BF16), pltpu.VMEM((state, length), BF16),
            pltpu.VMEM((length, state), BF16), pltpu.VMEM((length, state), BF16),
            pltpu.VMEM((length, length), F32), pltpu.VMEM((length, length), F32),
            pltpu.VMEM((length, 2 * state), BF16),
            states, states, states, states, *exchange, *exchange,
            pltpu.VMEM((4, heads, state), F32),
            dma, dma((2, XUNITS)), dma((2, XUNITS)), dma((2, ZUNITS)), dma((2, ZUNITS)),
            dma((15,)), dma((15,)), dma((2, 4, 7)), dma((2, 4, 7)), dma((3,)), dma((3,)),
        ],
        compiler_params=pltpu.CompilerParams(
            collective_id=0, has_side_effects=True, vmem_limit_bytes=60 << 20
        ),
    )(tokens[0], w_x.T, w_bc.T, w_dt.T, params, grad_y[0])
    return (y[None], dtok[None])


def solution(mesh):
    placed = (P("dp", "ctx", None), P(None, "dp"), P(), P(), P(), P(), P(), P("dp", "ctx", None))
    return jax.shard_map(
        local,
        mesh=mesh,
        in_specs=placed,
        out_specs=(P("dp", "ctx", None), P("dp", "ctx", None)),
        check_vma=False,
    )
```

time: 141 us -> 111 us (0.79)
  Pallas kernels: 133 us -> 102 us
    pallas_call x1, Pallas kernels: 133 us -> 102 us  [local(): pl.pallas_call(kernel, out_shape=(jax.ShapeDtypeStruct((length, hp), BF16...]
where the time goes in v2:
time: 111 us; the launch traced here: 110 us
  Pallas kernels  102 us (92%)
  local copies, waits for them, and re-layouts  6.77 us (6%)
    pallas_call x1, Pallas kernels, local(): pl.pallas_call(kernel, out_shape=(jax.ShapeDtypeStruct((length, hp), BF16...  102 us
    unnamed x5, local copies, waits for them, and re-layouts  6.04 us

profile of v2, /device:TPU:2, one launch (start us, length us, event | category | flops | bytes accessed | tf_op | source)
XLA Modules:
  0.0 109.8 jit_solution(16941146941056245005)
XLA Ops:
  0.6 0.7 pad_maximum_fusion
  1.3 0.7 broadcast_in_dim.12.par_ref
  2.1 2.4 %copy.10 = bf16[2560,256]{0,1:T(8,128)(2,1)} copy(bf16[2560,256]{1,0:T(8,128)(2,1)} %param.10) | data formatting | bytes 2621440 | tf_op args[2]
  4.5 101.7 %shard_map.95 = (bf16[256,2560]{1,0:T(8,128)(2,1)}, bf16[256,2560]{1,0:T(8,128)(2,1)}) custom-call(bf16[256,2560]{1,0:T(8,128)(2,1)} %bitcast.13, bf16[160,2560]{1,0:T(8,128)(2,1)} %bitcast.15, bf16[256,2560]{1,0:T(8,128)(2,1)} %bitcast.10, bf16[40,2560]{1,0:T(8,128)(2,1)} %bitcast.16, f32[3,40,256]{2,1,0:T(8,128)} %broadcast_in_dim.12.par_ref, ...), custom_call_target="tpu_custom_call" | custom-call | tf_op jit(solution)/shard_map/pallas_call | solution.py:617
  106.2 0.0 copy-start
  106.2 2.6 %copy.13 = bf16[1,256,2560]{2,1,0:T(8,128)(2,1)} copy(bf16[1,256,2560]{2,1,0:T(8,128)(2,1)} %bitcast.12) | data formatting | bytes 2621440
  108.7 0.0 copy-done
  108.7 1.1 copy.14
Async XLA Ops:
  106.2 2.6 %copy-start = (bf16[256,2560]{1,0:T(8,128)(2,1)S(1)}, bf16[256,2560]{1,0:T(8,128)(2,1)}, u32[]{:S(2)}) copy-start(bf16[256,2560]{1,0:T(8,128)(2,1)} %get-tuple-element.5) | copy-start | bytes 3932164

commit v3 on v2

--- a/solution.py
+++ b/solution.py
@@ -21,14 +21,17 @@
 PANEL = 160
 UNIT = 16
 HALF = 80
-XUNITS = 15
-ZUNITS = 20
-STEPS = 41
-GATHER = 28
-ENTER = (12, 22, 23, 28)
-LEAVE = (24, 35, 36, 40)
+XUNITS = 18
+XOWN = 15
+ZUNITS = 17
+LAG = 2
+STEPS = 33
+ENTER = (12, 22, 23, 25)
+LEAVE = (24, 28, 30, 32)
+INSIDE = ((17, 0, 1), (24, 1, 2), (26, 3, 1))
+PUSHED = (1, 2, 3)
 BLOCK = 32
-DTOK_FROM = 30
+DTOK_FROM = 27
 
 
 def mm(a, b, dims=NN):
@@ -36,14 +39,15 @@
 
 
 def kernel(
-    tok_ref, wt_in, wbc_ref, wdt_ref, par_ref, gy_ref,
+    tok_in, wt_in, wbc_in, wdt_ref, par_ref, gy_in,
     y_ref, dtok_ref,
-    wt, x_t, gy_t, xw, gw, gx_t, gx_n, y_t, acc_d, e_all, m_all,
+    tok_ref, wbc_ref, gy_ref, wt, x_t, gy_t, xw, gw, gx_t, gx_n, y_t, acc_d, e_all, m_all,
     run_s, step_s, sig_s, er_s, tail_s, left_s, a_own, q_s, acc_a, both_s,
     bt_s, ct_s, b_s, c_s, st_s, dst_s, gbc_s,
     s_loc, g_loc, ent, later, first_f, total_f, enter_f, pass_f, out_f,
     first_b, total_b, enter_b, pass_b, out_b, ay,
-    cp_sem, xs_s, xr_s, zs_s, zr_s, ds_s, dr_s, es_s, er_sem, as_s, ar_s,
+    az, push_f,
+    cp_sem, xs_s, xr_s, zs_s, zr_s, ds_s, dr_s, es_s, er_sem, as_s, ar_s, ps_s, pr_s,
 ):
     dp = lax.axis_index("dp")
     cx = lax.axis_index("ctx")
@@ -69,6 +73,9 @@
     def at_y(k):
         return (dp, zl * 4 + (y + k) % 4)
 
+    def at_zl(k):
+        return (dp, ((zl + k + 4) % 4) * 4 + y)
+
     sibling = (x * 4 + zh * 2 + (1 - c), cx)
 
     def remote(src, dst, send, recv, device):
@@ -81,12 +88,18 @@
         return ((xx % 4) * 4 + half * 2 + core) * PANEL
 
     own = pl.multiple_of(panel_row(x, zh, c), UNIT)
-    cp = pltpu.make_async_copy(wt_in, wt.at[pl.ds(own, PANEL)], cp_sem)
+    cp = pltpu.make_async_copy(wt_in, wt.at[pl.ds(own, PANEL)], cp_sem.at[0])
+    loads = [
+        pltpu.make_async_copy(src, dst, cp_sem.at[i + 1])
+        for i, (src, dst) in enumerate(((tok_in, tok_ref), (wbc_in, wbc_ref), (gy_in, gy_ref)))
+    ]
     cp.start()
+    for load in loads:
+        load.start()
 
     barrier = pltpu.get_barrier_semaphore()
     peers = [at_x(1), at_x(3), at_z(1), at_z(-1), sibling]
-    peers += [at_y(k) for k in (1, 2, 3)]
+    peers += [at_y(k) for k in (1, 2, 3)] + [at_zl(k) for k in (1, 2, 3)]
     for peer in peers:
         pl.semaphore_signal(barrier, inc=1, device_id=peer, device_id_type=MESH)
     pl.semaphore_wait(barrier, len(peers))
@@ -99,19 +112,27 @@
         if way == 0:
             start = jnp.where(
                 j < 10, panel_row(x, zh, c) + UNIT * j,
-                panel_row(x + 1, zh, c) + UNIT * (j - 10),
+                jnp.where(
+                    j < XOWN, panel_row(x + 1, zh, c) + UNIT * (j - 10),
+                    panel_row(x + 1, 1 - zh, c) + UNIT * (j - 13),
+                ),
             )
             device = at_x(3)
         else:
             start = jnp.where(
                 j < 10, panel_row(x, zh, c) + UNIT * ((j + 5) % 10),
-                panel_row(x + 3, zh, c) + UNIT * (j - 5),
+                jnp.where(
+                    j < XOWN, panel_row(x + 3, zh, c) + UNIT * (j - 5),
+                    panel_row(x + 3, 1 - zh, c) + HALF + UNIT * (j - 13),
+                ),
             )
             device = at_x(1)
         ref = rows(start, UNIT)
         return remote(ref, ref, xs_s.at[way, j], xr_s.at[way, j], device)
 
     def order(way, g):
+        if isinstance(g, int):
+            return ((0, 1, 3, 2), (0, 3, 1, 2))[way][g]
         if way == 0:
             return jnp.where(g == 2, 3, jnp.where(g == 3, 2, g))
         return jnp.where(g == 1, 3, jnp.where(g == 2, 1, jnp.where(g == 3, 2, 0)))
@@ -160,30 +181,40 @@
                 z_copy(way, k).start()
     sib_own().start()
 
-    tok = tok_ref[...]
-    bc_t = mm(wbc_ref[...], tok, NT)
-    nstate = bc_t.shape[0] // 2
-    bt_s[...] = bc_t[:nstate].astype(BF16)
-    ct_s[...] = bc_t[nstate:].astype(BF16)
-    b_s[...] = bc_t[:nstate].T.astype(BF16)
-    c_s[...] = bc_t[nstate:].T.astype(BF16)
-    raw = mm(wdt_ref[...], tok, NT)[:nhead]
-    length = raw.shape[1]
-    shifted = raw + par_ref[0]
-    step = jnp.maximum(shifted, 0.0) + jnp.log1p(jnp.exp(-jnp.abs(shifted)))
-    step_s[...] = step
-    sig_s[...] = 1.0 / (1.0 + jnp.exp(-shifted))
+    nstate = bt_s.shape[0]
+    nhead, length = run_s.shape
     first = lax.broadcasted_iota(jnp.int32, (length, length), 0)
     second = lax.broadcasted_iota(jnp.int32, (length, length), 1)
-    upper = jnp.where(first <= second, 1.0, 0.0)
-    run = lax.dot_general(-par_ref[1] * step, upper, NN, precision=HI, preferred_element_type=F32)
-    run_s[...] = run
-    er_s[...] = jnp.exp(run)
-    last = run[:, length - 1 :]
-    left_s[...] = jnp.exp(last - run)
-    tail_s[...] = left_s[...] * step
-    a_own[...] = jnp.broadcast_to(jnp.exp(last), a_own.shape)
-    st_s[...] = mm(b_s[...], ct_s[...])
+
+    def readouts():
+        loads[0].wait()
+        loads[1].wait()
+        bc_t = mm(tok_ref[...], wbc_ref[...]).T
+        bt_s[...] = bc_t[:nstate].astype(BF16)
+        ct_s[...] = bc_t[nstate:].astype(BF16)
+        b_s[...] = bc_t[:nstate].T.astype(BF16)
+        c_s[...] = bc_t[nstate:].T.astype(BF16)
+
+    def rates():
+        shifted = mm(wdt_ref[...], tok_ref[...], NT)[:nhead] + par_ref[0]
+        step = jnp.maximum(shifted, 0.0) + jnp.log1p(jnp.exp(-jnp.abs(shifted)))
+        step_s[...] = step
+        sig_s[...] = 1.0 / (1.0 + jnp.exp(-shifted))
+        upper = jnp.where(first <= second, 1.0, 0.0)
+        run = lax.dot_general(
+            -par_ref[1] * step, upper, NN, precision=HI, preferred_element_type=F32
+        )
+        run_s[...] = run
+        er_s[...] = jnp.exp(run)
+        last = run[:, length - 1 :]
+        left_s[...] = jnp.exp(last - run)
+        tail_s[...] = left_s[...] * step
+        a_own[...] = jnp.broadcast_to(jnp.exp(last), a_own.shape)
+        for k in (1, 2, 3):
+            a_y(k).start()
+        ay[y] = a_own[...]
+        st_s[...] = mm(b_s[...], ct_s[...])
+        loads[2].wait()
 
     def two(ref, q):
         return jnp.concatenate(
@@ -196,9 +227,8 @@
     def a_y(k):
         return remote(a_own, ay.at[y], as_s.at[k - 1], ar_s.at[k - 1], at_y(k))
 
-    for k in (1, 2, 3):
-        a_y(k).start()
-    ay[y] = a_own[...]
+    def a_z(k):
+        return remote(az.at[zl], az.at[zl], as_s.at[k + 2], ar_s.at[k + 2], at_zl(k))
 
     def head_rows(h):
         return pl.ds(pl.multiple_of(h * HEAD, HEAD), HEAD)
@@ -233,6 +263,11 @@
             at_z(1) if way == 0 else at_z(-1),
         )
 
+    def e_push(g, k):
+        return remote(
+            pass_f.at[g], push_f.at[g, zl], ps_s.at[g, k - 1], pr_s.at[g, k - 1], at_zl(k)
+        )
+
     def e_back(way, g, k):
         return remote(
             out_of[way].at[g, (y + k) % 4], res_of[way].at[slice_at(way, g, 0)],
@@ -266,6 +301,13 @@
             total_of[way][g, at, :] = t
             pass_of[way][g, at, :] = t.astype(BF16)
 
+        if way == 0 and g in PUSHED:
+            for k in (1, 2, 3):
+                @pl.when(zl + k < 4)
+                def _():
+                    e_push(g, k).start()
+            return
+
         @pl.when(starts[way])
         def _():
             e_pass(way, g).start()
@@ -288,6 +330,29 @@
 
                 e_pass(way, g).start()
 
+        spread(way, g)
+
+    def collect(g):
+        for k in (1, 2, 3):
+            @pl.when(zl - k >= 0)
+            def _():
+                e_push(g, k).wait_recv()
+
+        @pl.loop(0, slice_rows // BLOCK)
+        def _(b):
+            at = block_rows(b)
+            h = group_base(0, g) // HEAD + (y * slice_rows + b * BLOCK) // HEAD
+            total_f[g, at, :] = jnp.zeros((BLOCK, nstate), F32)
+            for s in range(3):
+                @pl.when(s < zl)
+                def _():
+                    e = az[s, pl.ds(h, 1), :] * total_f[g, at, :]
+                    total_f[g, at, :] = e + push_f[g, s, at, :].astype(F32)
+            enter_f[g, at, :] = total_f[g, at, :].astype(BF16)
+
+        spread(0, g)
+
+    def spread(way, g):
         @pl.loop(0, slice_rows // BLOCK)
         def _(b):
             at = block_rows(b)
@@ -312,6 +377,13 @@
             e_first(way, g, k).wait_send()
             e_back(way, g, k).wait_send()
 
+        if way == 0 and g in PUSHED:
+            for k in (1, 2, 3):
+                @pl.when(zl + k < 4)
+                def _():
+                    e_push(g, k).wait_send()
+            return
+
         @pl.when(jnp.logical_not(ends[way]))
         def _():
             e_pass(way, g).wait_send()
@@ -341,11 +413,14 @@
         e_all[h, :side, :side] = e00.astype(BF16)
         e_all[h, :side, side:] = e01.astype(BF16)
         e_all[h, side:, side:] = e11.astype(BF16)
-        m_all[h, :side, :side] = (e00 * st_s[:side, :side]).astype(BF16)
-        m_all[h, :side, side:] = (e01 * st_s[:side, side:]).astype(BF16)
-        m_all[h, side:, :side] = jnp.zeros((side, side), BF16)
-        m_all[h, side:, side:] = (e11 * st_s[side:, side:]).astype(BF16)
-        gx_t[at, :] = mm(gy_t[at, :], m_all[h], NT)
+        m00 = (e00 * st_s[:side, :side]).astype(BF16)
+        m01 = (e01 * st_s[:side, side:]).astype(BF16)
+        m11 = (e11 * st_s[side:, side:]).astype(BF16)
+        upper = jnp.concatenate([m00, m01], axis=1)
+        lower = jnp.concatenate([jnp.zeros_like(m11), m11], axis=1)
+        m = jnp.concatenate([upper, lower], axis=0)
+        m_all[h] = m
+        gx_t[at, :] = mm(gy_t[at, :], m, NT)
 
     def pull_back(q):
         at = pair_rows(q)
@@ -359,8 +434,7 @@
         at = pl.ds(pl.multiple_of(base, group), group)
         x_t[at, :] = mm(wt[at, :], tok_ref[...], NT).astype(BF16)
 
-        @pl.loop(0, group_pairs)
-        def _(i):
+        for i in range(group_pairs):
             q = base // PAIR + i
             here = pair_rows(q)
             scaled = (x_t[here, :].astype(F32) * two(tail_s, q)).astype(BF16)
@@ -403,153 +477,191 @@
         return pl.ds(pl.multiple_of(n * wide, 128), wide)
 
     def pick(s, table):
+        if isinstance(s, int):
+            return table.index(s) if s in table else -1
         found = -1
         for i, t in enumerate(table):
             found = jnp.where(s == t, i, found)
         return found
 
-    @pl.loop(0, STEPS)
-    def _(s):
+    def when(condition):
+        def run(body):
+            if not isinstance(condition, bool):
+                pl.when(condition)(body)
+            elif condition:
+                body()
+
+        return run
+
+    def step(s):
         j = s - 2
 
-        @pl.when((j >= 0) & (j < XUNITS))
+        @when(0 <= j < XOWN)
         def _():
             for way in (0, 1):
                 x_copy(way, j).wait_recv()
 
-            @pl.when(j < 5)
+            @when(j < 5)
             def _():
                 for way in (0, 1):
                     x_copy(way, j + 10).start()
 
             for way in (0, 1):
-                @pl.when(is_source[way])
+                @when(is_source[way] if j + 5 < ZUNITS else False)
                 def _():
                     z_copy(way, j + 5).start()
 
-            @pl.when(j % 5 == 4)
+            @when(j % 5 == 4)
             def _():
                 for way in (0, 1):
                     sib_x(way, j // 5).start()
 
         for way in (0, 1):
-            k = s - 2 - 2 * (zl if way == 0 else 3 - zl)
-
-            @pl.when((k >= 0) & (k < ZUNITS))
+            away = LAG * (zl if way == 0 else 3 - zl)
+            late = s - 4 - away
+
+            @when((late >= 7) & (late < 10))
+            def _():
+                x_copy(way, late + 8).wait_recv()
+
+            k = s - 2 - away
+
+            @when((k >= 0) & (k < ZUNITS))
             def _():
                 z_copy(way, k).wait_recv()
 
-                @pl.when(jnp.logical_not(is_source[way]))
+                @when(jnp.logical_not(is_source[way]))
                 def _():
                     z_copy(way, k).start()
 
-                @pl.when(k % 5 == 4)
+                @when((k >= 7) & (k < 10))
+                def _():
+                    x_copy(way, k + 8).start()
+
+                @when((k % 5 == 4) | (k == ZUNITS - 1))
                 def _():
                     sib_z(way, k // 5).start()
 
-        @pl.when(s == 2)
+        @when(s == 5)
         def _():
             for k in (1, 2, 3):
                 a_y(k).wait()
-
-        b = s - 3
-
-        @pl.when((b >= 0) & (b < 4))
+            az[zl] = ay[0] * ay[1] * ay[2] * ay[3]
+            for k in (1, 2, 3):
+                a_z(k).start()
+
+        @when(s == 10)
+        def _():
+            for k in (1, 2, 3):
+                a_z(k).wait()
+
+        b = s - 7
+
+        @when((b >= 0) & (b < 4))
         def _():
             totals(1, b)
 
-        b = s - 4 - 2 * (3 - zl)
-
-        @pl.when((b >= 0) & (b < 4))
+        b = s - 8 - 2 * (3 - zl)
+
+        @when((b >= 0) & (b < 4))
         def _():
             chain(1, b)
 
         g_total = pick(s - 2, ENTER)
 
-        @pl.when(g_total >= 0)
+        @when(g_total >= 0)
         def _():
             totals(0, g_total)
 
-        g_chain = pick(s - 3 - 2 * zl, ENTER)
-
-        @pl.when(g_chain >= 0)
-        def _():
-            chain(0, g_chain)
+        @when((s >= ENTER[0] + 3) & (s - 3 - 2 * zl == ENTER[0]) if s < ENTER[0] + 10 else False)
+        def _():
+            chain(0, 0)
+
+        g_push = pick(s - 4, ENTER)
+
+        @when(g_push in PUSHED)
+        def _():
+            collect(g_push)
 
         g_enter = pick(s, ENTER)
 
-        @pl.when(g_enter >= 0)
-        def _():
-            @pl.when(g_enter == 0)
+        @when(g_enter >= 0)
+        def _():
+            @when(g_enter == 0)
             def _():
                 sib_own().wait_recv()
 
-            @pl.when(g_enter > 0)
-            def _():
-                sib_copy(jnp.where(g_enter == 3, 4, g_enter - 1), 0, HALF).wait_recv()
-                sib_copy(jnp.where(g_enter == 3, 5, g_enter + 1), 0, HALF).wait_recv()
-
-            swapped = jnp.where(g_enter == 1, 2, jnp.where(g_enter == 2, 1, g_enter))
+            @when(g_enter > 0)
+            def _():
+                sib_copy(4 if g_enter == 3 else g_enter - 1, 0, HALF).wait_recv()
+                sib_copy(5 if g_enter == 3 else g_enter + 1, 0, HALF).wait_recv()
+
+            swapped = (0, 2, 1, 3)[g_enter]
             sib_copy(6 + 2 * g_enter, 0, HALF).wait_recv()
             sib_copy(7 + 2 * swapped, 0, HALF).wait_recv()
             project(g_enter)
             begin(0, g_enter)
 
-        @pl.when(s < 4)
-        def _():
-            @pl.loop(0, group_pairs)
-            def _(i):
-                own_states(s * group_pairs + i)
-
-            begin(1, s)
-
-        @pl.when((s >= 4) & (s < 14))
-        def _():
-            @pl.loop(0, 4)
-            def _(i):
-                mixing((s - 4) * 4 + i)
-
-        b = s - 13
-
-        @pl.when((b >= 0) & (b < 4))
+        @when(s == 0)
+        def _():
+            readouts()
+
+        @when(s == 2)
+        def _():
+            rates()
+
+        @when(4 <= s < 8)
+        def _():
+            for i in range(group_pairs):
+                own_states((s - 4) * group_pairs + i)
+
+            begin(1, s - 4)
+
+        @when(8 <= s < 16)
+        def _():
+            for i in range(nhead // 8):
+                mixing((s - 8) * (nhead // 8) + i)
+
+        b = s - 17
+
+        @when((b >= 0) & (b < 4))
         def _():
             finish(1, b)
 
-            @pl.loop(0, group_pairs)
-            def _(i):
+            for i in range(group_pairs):
                 pull_back(b * group_pairs + i)
 
         def inside_some(first_step, g0, count):
             per = group_heads * count // 5
             n = s - first_step
 
-            @pl.when((n >= 0) & (n < 5))
-            def _():
-                @pl.loop(0, per)
-                def _(i):
+            @when(0 <= n < 5)
+            def _():
+                for i in range(per):
                     e = n * per + i
                     g = g0 + e // group_heads
                     inside(group_base(0, g) // HEAD + e % group_heads)
 
-        inside_some(17, 0, 1)
-        inside_some(24, 1, 2)
-        inside_some(29, 3, 1)
+        for some in INSIDE:
+            inside_some(*some)
 
         n = s - DTOK_FROM
 
-        @pl.when((n >= 0) & (n < 5))
+        @when(0 <= n < 5)
         def _():
             acc_d[:, columns(n)] = mm(gx_n[...], wt[:, columns(n)])
 
         g_leave = pick(s, LEAVE)
 
-        @pl.when(g_leave >= 0)
+        @when(g_leave >= 0)
         def _():
             finish(0, g_leave)
 
-            @pl.loop(0, group_pairs)
-            def _(i):
+            for i in range(group_pairs):
                 outputs(group_base(0, g_leave) // PAIR + i)
+
+    for s in range(STEPS):
+        step(s)
 
     dst = dst_s[...].astype(BF16)
     gb_t = mm(ct_s[...], dst, NT) + mm(later[...], xw[...], TN)
@@ -566,7 +678,7 @@
     @pl.loop(0, 5)
     def _(n):
         at = columns(n)
-        total = acc_d[:, at] + mm(gbc_s[...], wbc_ref[:, at])
+        total = acc_d[:, at] + mm(gbc_s[...], wbc_ref[at, :], NT)
         total = total + mm(g_raw, wdt_ref[:nhead, at], TN)
         dtok_ref[:, at] = total.astype(BF16)
 
@@ -588,8 +700,7 @@
         for way in (0, 1):
             z_copy(way, k).wait_send()
 
-    @pl.loop(0, 4)
-    def _(g):
+    for g in range(4):
         for way in (0, 1):
             drain(way, g)
 
@@ -604,6 +715,7 @@
         jnp.stack([dt_bias, decay_rate, skip_gain])[:, :, None], (3, heads, length)
     )
     vmem = pl.BlockSpec(memory_space=pltpu.VMEM)
+    hbm = pl.BlockSpec(memory_space=pl.ANY)
     flat = pltpu.VMEM((hp, length), BF16)
     wide = pltpu.VMEM((hp, length), F32)
     per_head = pltpu.VMEM((heads, length), F32)
@@ -620,9 +732,11 @@
             jax.ShapeDtypeStruct((length, hp), BF16),
             jax.ShapeDtypeStruct((length, width), BF16),
         ),
-        in_specs=[vmem] * 6,
+        in_specs=[hbm, hbm, hbm, vmem, vmem, hbm],
         out_specs=(vmem, vmem),
         scratch_shapes=[
+            pltpu.VMEM((length, width), BF16), pltpu.VMEM((width, 2 * state), BF16),
+            pltpu.VMEM((length, hp), BF16),
             pltpu.VMEM((hp, width), BF16), flat, flat, flat, flat, wide,
             pltpu.VMEM((length, hp), BF16), wide, pltpu.VMEM((length, width), F32),
             pltpu.VMEM((heads, length, length), BF16), pltpu.VMEM((heads, length, length), BF16),
@@ -633,14 +747,15 @@
             pltpu.VMEM((length, length), F32), pltpu.VMEM((length, length), F32),
             pltpu.VMEM((length, 2 * state), BF16),
             states, states, states, states, *exchange, *exchange,
-            pltpu.VMEM((4, heads, state), F32),
-            dma, dma((2, XUNITS)), dma((2, XUNITS)), dma((2, ZUNITS)), dma((2, ZUNITS)),
-            dma((15,)), dma((15,)), dma((2, 4, 7)), dma((2, 4, 7)), dma((3,)), dma((3,)),
+            pltpu.VMEM((4, heads, state), F32), pltpu.VMEM((4, heads, state), F32), slots,
+            dma((4,)), dma((2, XUNITS)), dma((2, XUNITS)), dma((2, ZUNITS)), dma((2, ZUNITS)),
+            dma((15,)), dma((15,)), dma((2, 4, 7)), dma((2, 4, 7)), dma((6,)), dma((6,)),
+            dma((4, 3)), dma((4, 3)),
         ],
         compiler_params=pltpu.CompilerParams(
             collective_id=0, has_side_effects=True, vmem_limit_bytes=60 << 20
         ),
-    )(tokens[0], w_x.T, w_bc.T, w_dt.T, params, grad_y[0])
+    )(tokens[0], w_x.T, w_bc, w_dt.T, params, grad_y[0])
     return (y[None], dtok[None])
 
 

time: 111 us -> 101 us (0.910)
  Pallas kernels: 102 us -> 94.5 us
  local copies, waits for them, and re-layouts: 6.77 us -> 4.35 us
    pallas_call x1, Pallas kernels: 102 us -> 94.5 us  [local(): pl.pallas_call(kernel, out_shape=(jax.ShapeDtypeStruct((length, hp), BF16...]
    unnamed x5 -> x4, local copies, waits for them, and re-layouts: 6.04 us -> 3.62 us
where the time goes in v3:
time: 101 us; the launch traced here: 100 us
  Pallas kernels  94.5 us (94%)
  local copies, waits for them, and re-layouts  4.35 us (4%)
    pallas_call x1, Pallas kernels, local(): pl.pallas_call(kernel, out_shape=(jax.ShapeDtypeStruct((length, hp), BF16...  94.5 us
    unnamed x4, local copies, waits for them, and re-layouts  3.62 us

profile of v3, /device:TPU:2, one launch (start us, length us, event | category | flops | bytes accessed | tf_op | source)
XLA Modules:
  0.0 100.2 jit_solution(11562067382986078000)
XLA Ops:
  0.6 0.7 pad_maximum_fusion
  1.3 0.7 broadcast_in_dim.12.par_ref
  2.1 94.5 %shard_map.95 = (bf16[256,2560]{1,0:T(8,128)(2,1)}, bf16[256,2560]{1,0:T(8,128)(2,1)}) custom-call(bf16[256,2560]{1,0:T(8,128)(2,1)} %bitcast.11, bf16[160,2560]{1,0:T(8,128)(2,1)} %bitcast.13, bf16[2560,256]{1,0:T(8,128)(2,1)} %wbc_in.1, bf16[40,2560]{1,0:T(8,128)(2,1)} %bitcast.14, f32[3,40,256]{2,1,0:T(8,128)} %broadcast_in_dim.12.par_ref, ...), custom_call_target="tpu_custom_call" | custom-call | tf_op jit(solution)/shard_map/pallas_call | solution.py:729
  96.6 0.0 copy-start
  96.6 2.6 %copy.12 = bf16[1,256,2560]{2,1,0:T(8,128)(2,1)} copy(bf16[1,256,2560]{2,1,0:T(8,128)(2,1)} %bitcast.10) | data formatting | bytes 2621440
  99.2 0.0 copy-done
  99.2 1.1 %copy.13 = bf16[1,256,2560]{2,1,0:T(8,128)(2,1)} copy(bf16[1,256,2560]{2,1,0:T(8,128)(2,1)S(1)} %bitcast.9) | data formatting | bytes 2621440
Async XLA Ops:
  96.6 2.6 %copy-start = (bf16[256,2560]{1,0:T(8,128)(2,1)S(1)}, bf16[256,2560]{1,0:T(8,128)(2,1)}, u32[]{:S(2)}) copy-start(bf16[256,2560]{1,0:T(8,128)(2,1)} %get-tuple-element.5) | copy-start | bytes 3932164

commit v4 on v3

--- a/solution.py
+++ b/solution.py
@@ -25,6 +25,7 @@
 XOWN = 15
 ZUNITS = 17
 LAG = 2
+AHEAD = 3
 STEPS = 33
 ENTER = (12, 22, 23, 25)
 LEAVE = (24, 28, 30, 32)
@@ -168,7 +169,7 @@
         ref = rows(own, PANEL)
         return remote(ref, ref, ds_s.at[14], dr_s.at[14], sibling)
 
-    @pl.loop(0, 10)
+    @pl.loop(0, AHEAD)
     def _(j):
         x_copy(0, j).start()
         x_copy(1, j).start()
@@ -176,7 +177,7 @@
     for way in (0, 1):
         @pl.when(is_source[way])
         def _():
-            @pl.loop(0, 5)
+            @pl.loop(0, AHEAD)
             def _(k):
                 z_copy(way, k).start()
     sib_own().start()
@@ -501,15 +502,15 @@
             for way in (0, 1):
                 x_copy(way, j).wait_recv()
 
-            @when(j < 5)
+            @when(j + AHEAD < XOWN)
             def _():
                 for way in (0, 1):
-                    x_copy(way, j + 10).start()
+                    x_copy(way, j + AHEAD).start()
 
             for way in (0, 1):
-                @when(is_source[way] if j + 5 < ZUNITS else False)
+                @when(is_source[way] if j + AHEAD < ZUNITS else False)
                 def _():
-                    z_copy(way, j + 5).start()
+                    z_copy(way, j + AHEAD).start()
 
             @when(j % 5 == 4)
             def _():

time: 101 us -> 96.9 us (0.959)
  Pallas kernels: 94.5 us -> 90.7 us
    pallas_call x1, Pallas kernels: 94.5 us -> 90.7 us  [local(): pl.pallas_call(kernel, out_shape=(jax.ShapeDtypeStruct((length, hp), BF16...]
where the time goes in v4:
time: 96.9 us; the launch traced here: 96.4 us
  Pallas kernels  90.7 us (94%)
  local copies, waits for them, and re-layouts  4.35 us (4%)
    pallas_call x1, Pallas kernels, local(): pl.pallas_call(kernel, out_shape=(jax.ShapeDtypeStruct((length, hp), BF16...  90.7 us
    unnamed x4, local copies, waits for them, and re-layouts  3.62 us

profile of v4, /device:TPU:2, one launch (start us, length us, event | category | flops | bytes accessed | tf_op | source)
XLA Modules:
  0.0 96.4 jit_solution(17784892638273478254)
XLA Ops:
  0.6 0.7 pad_maximum_fusion
  1.3 0.7 broadcast_in_dim.12.par_ref
  2.1 90.7 %shard_map.95 = (bf16[256,2560]{1,0:T(8,128)(2,1)}, bf16[256,2560]{1,0:T(8,128)(2,1)}) custom-call(bf16[256,2560]{1,0:T(8,128)(2,1)} %bitcast.11, bf16[160,2560]{1,0:T(8,128)(2,1)} %bitcast.13, bf16[2560,256]{1,0:T(8,128)(2,1)} %wbc_in.1, bf16[40,2560]{1,0:T(8,128)(2,1)} %bitcast.14, f32[3,40,256]{2,1,0:T(8,128)} %broadcast_in_dim.12.par_ref, ...), custom_call_target="tpu_custom_call" | custom-call | tf_op jit(solution)/shard_map/pallas_call | solution.py:730
  92.8 0.0 copy-start
  92.8 2.6 %copy.12 = bf16[1,256,2560]{2,1,0:T(8,128)(2,1)} copy(bf16[1,256,2560]{2,1,0:T(8,128)(2,1)} %bitcast.10) | data formatting | bytes 2621440
  95.3 0.0 copy-done
  95.3 1.1 %copy.13 = bf16[1,256,2560]{2,1,0:T(8,128)(2,1)} copy(bf16[1,256,2560]{2,1,0:T(8,128)(2,1)S(1)} %bitcast.9) | data formatting | bytes 2621440
Async XLA Ops:
  92.8 2.6 %copy-start = (bf16[256,2560]{1,0:T(8,128)(2,1)S(1)}, bf16[256,2560]{1,0:T(8,128)(2,1)}, u32[]{:S(2)}) copy-start(bf16[256,2560]{1,0:T(8,128)(2,1)} %get-tuple-element.5) | copy-start | bytes 3932164
